TPU v7x, 256 devices: a whole 4x4x8 slice. The times are simulated.
256 devices in a mesh: gx: 64 (over z, y, x_hi), gy: 4 (over x_lo, core).
Axes of the slice: x: 4 (x_hi: 2, x_lo: 2; x = x_hi * 2 + x_lo), y: 4, z: 8, core: 2. Of those that a mesh axis runs over, the one named last changes fastest.
Arguments:
- points: bfloat16 [4, 64, 64, 32, 128], P('gy', 'gx'), may hold values from -6 to 6
- counts: int32 [4, 64, 64], P('gy', 'gx'), may hold values from 10 to 32, as said below
- voxels: int32 [4, 64, 64, 32], P('gy', 'gx'), may hold values from 0 to 1023, as said below
- occupancy: int32 [64, 4, 2], P('gx', 'gy'), may hold values from 0 to 1, as said below
- weight: bfloat16 [27, 96, 96], replicated, may hold values from -0.125 to 0.125
- w_in: bfloat16 [128, 96], replicated, may hold values from -0.5 to 0.5
- cotangent: bfloat16 [512, 32, 16, 96], P('gx', 'gy'), may hold values from -6 to 6
Outputs:
- point_feat: bfloat16 [4, 64, 64, 32, 96], P('gy', 'gx')
- point_grad: bfloat16 [4, 64, 64, 32, 128], P('gy', 'gx')
- weight_grad: float32 [27, 96, 96], replicated
Inputs may be any that keep to these rules, and one draw needn't show every extreme that they name: `counts`: in each gy row one owner receives 32 rows from every source. `voxels`: every slot's voxel lies in an occupied block of its owner tile. `occupancy`: every tile has at least one occupied block.
All inputs are finite; a program needn't handle non-finite values.
Results may differ from a plain program's by a relative error of at most 0.01.
Values may be sent and summed in bfloat16 or wider, within the bound.
A program may use at most 64 MiB of HBM per device.

v0:
```python
import jax
import jax.numpy as jnp
from jax import lax
from jax.sharding import PartitionSpec as P


def padded_2(block, sides, width):
    for axis, dim in sides:
        count = lax.axis_size(axis)
        forward = [(i, i + 1) for i in range(count - 1)]
        backward = [(target, source) for source, target in forward]
        low = lax.ppermute(
            lax.slice_in_dim(block, block.shape[dim] - width, None, axis=dim), axis, forward
        )
        high = lax.ppermute(lax.slice_in_dim(block, 0, width, axis=dim), axis, backward)
        block = jnp.concatenate([low, block, high], axis=dim)
    return block


def pad_depth(field):
    return jnp.pad(field, ((0, 0), (0, 0), (1, 1), (0, 0)))


def forward_taps(padded, weight, depth, width):
    total = jnp.zeros((64 * depth, width), jnp.float32)
    for tap in range(27):
        a, b, c = (tap // 9, tap // 3 % 3, tap % 3)
        window = padded[a : a + 8, b : b + 8, c : c + depth].reshape(-1, width)
        total = total + jnp.dot(window, weight[tap], preferred_element_type=jnp.float32)
    return total


def weight_terms(padded, grad_flat, depth, width):
    terms = []
    for tap in range(27):
        a, b, c = (tap // 9, tap // 3 % 3, tap % 3)
        window = padded[a : a + 8, b : b + 8, c : c + depth].reshape(-1, width)
        terms.append(
            lax.dot_general(
                window, grad_flat, (((0,), (0,)), ((), ())), preferred_element_type=jnp.float32
            )
        )
    return jnp.stack(terms)


def backward_taps(padded, weight, depth, width):
    total = jnp.zeros((64 * depth, width), jnp.float32)
    for tap in range(27):
        a, b, c = (tap // 9, tap // 3 % 3, tap % 3)
        window = padded[2 - a : 10 - a, 2 - b : 10 - b, 2 - c : 2 - c + depth].reshape(-1, width)
        total = total + jnp.dot(window, weight[tap].T, preferred_element_type=jnp.float32)
    return total


def on_device(points, counts, voxels, occupancy, weight, w_in, cotangent):
    width = weight.shape[2]
    feat_width = points.shape[4]
    depth = cotangent.shape[2]
    shape_slots = voxels.shape
    slots = lax.broadcasted_iota(jnp.int32, shape_slots, 3)
    got_points, got_voxels, got_counts = (
        lax.all_to_all(points, "gx", split_axis=2, concat_axis=2, tiled=True),
        lax.all_to_all(voxels, "gx", split_axis=2, concat_axis=2, tiled=True),
        lax.all_to_all(counts, "gx", split_axis=2, concat_axis=2, tiled=True),
    )
    got_valid = (slots < got_counts[..., None]).astype(jnp.float32).reshape(-1, 1)
    proj = (
        jnp.dot(got_points.reshape(-1, feat_width), w_in, preferred_element_type=jnp.float32)
        * got_valid
    ).astype(jnp.bfloat16)
    flat_index = got_voxels.reshape(-1)
    column_mask = jnp.repeat(occupancy[0, 0], 8).astype(jnp.float32)
    mask = jnp.broadcast_to(column_mask[None, None, :, None], (8, 8, depth, 1))
    summed = (
        jnp.zeros((64 * depth, width), jnp.float32).at[flat_index].add(proj.astype(jnp.float32))
    )
    feature = (summed.reshape(8, 8, depth, width) * mask).astype(jnp.bfloat16)
    grad_masked = (cotangent.astype(jnp.float32) * mask).astype(jnp.bfloat16)
    feature_pad = pad_depth(padded_2(feature, (("gx", 0), ("gy", 1)), 1))
    grad_pad = pad_depth(padded_2(grad_masked, (("gx", 0), ("gy", 1)), 1))
    mask_flat = mask.reshape(-1, 1)
    output = (forward_taps(feature_pad, weight, depth, width) * mask_flat).astype(jnp.bfloat16)
    local_grad = weight_terms(feature_pad, grad_masked.reshape(-1, width), depth, width)
    weight_grad = lax.psum(local_grad, ("gx", "gy"))
    feature_grad = (backward_taps(grad_pad, weight, depth, width) * mask_flat).astype(jnp.bfloat16)
    out_rows = (output[flat_index].astype(jnp.float32) * got_valid).astype(jnp.bfloat16)
    grad_rows = feature_grad[flat_index]
    point_rows = jnp.dot(grad_rows, w_in.T, preferred_element_type=jnp.float32) * got_valid
    sent_point = point_rows.astype(jnp.bfloat16).reshape(shape_slots + (feat_width,))
    point_feat, point_grad = (
        lax.all_to_all(
            out_rows.reshape(shape_slots + (width,)), "gx", split_axis=2, concat_axis=2, tiled=True
        ),
        lax.all_to_all(sent_point, "gx", split_axis=2, concat_axis=2, tiled=True),
    )
    return (point_feat, point_grad, weight_grad)


def solution(mesh):
    placed = (
        P("gy", "gx", None, None, None),
        P("gy", "gx", None),
        P("gy", "gx", None, None),
        P("gx", "gy", None),
        P(),
        P(),
        P("gx", "gy", None, None),
    )
    return jax.shard_map(
        on_device,
        mesh=mesh,
        in_specs=placed,
        out_specs=(P("gy", "gx", None, None, None), P("gy", "gx", None, None, None), P()),
        check_vma=False,
    )
```

profile of v0, /device:TPU:1, one launch (start us, length us, event | category | flops | bytes accessed | tf_op | source)
XLA Modules:
  0.0 468.1 jit_solution(846735209724311216)
XLA Ops:
  7.2 1.4 copy.31
  8.5 15.1 %all-to-all-start.2 = ((s32[1,1,64]{1,0,2:T(1,128)}), s32[1,1,64]{1,0,2:T(1,128)S(1)}, u32[]{:S(2)}, u32[]{:S(2)}) async-start(s32[1,1,64]{1,0,2:T(1,128)} %copy.31), calls=%async_computation.2 | async-start | bytes 65536 | tf_op jit(solution)/shard_map/all_to_all | solution.py:64
  23.7 1.4 copy.29
  25.1 9.3 %all-to-all-done.2 = s32[1,1,64]{1,0,2:T(1,128)S(1)} async-done(((s32[1,1,64]{1,0,2:T(1,128)}), s32[1,1,64]{1,0,2:T(1,128)S(1)}, u32[]{:S(2)}, u32[]{:S(2)}) %all-to-all-start.2) | async-done | bytes 288 | tf_op jit(solution)/shard_map/all_to_all | solution.py:64
  34.4 4.6 all-to-all-start
  39.0 0.7 convert_bitcast_fusion
  40.0 1.2 reduce.1
  41.4 8.4 %all-to-all-done = s32[1,1,64,32]{3,1,0,2:T(1,128)S(1)} async-done(((s32[1,1,64,32]{3,1,0,2:T(1,128)}), s32[1,1,64,32]{3,1,0,2:T(1,128)S(1)}, u32[]{:S(2)}, u32[]{:S(2)}) %all-to-all-start) | async-done | bytes 8224 | tf_op jit(solution)/shard_map/all_to_all | solution.py:63
  49.8 4.6 all-to-all-start.1
  54.5 0.5 broadcast.138
  55.0 0.7 reduce.4
  55.9 13.2 %all-to-all-done.1 = bf16[1,1,64,32,128]{4,3,1,0,2:T(8,128)(2,1)S(1)} async-done(((bf16[1,1,64,32,128]{4,3,1,0,2:T(8,128)(2,1)}), bf16[1,1,64,32,128]{4,3,1,0,2:T(8,128)(2,1)S(1)}, u32[]{:S(2)}, u32[]{:S(2)}) %all-to-all-start.1) | async-done | bytes 524320 | tf_op jit(solution)/shard_map/all_to_all | solution.py:62
  69.8 11.6 %scatter_custom_fusion = f32[1024,96]{1,0:T(8,128)S(1)} fusion(s32[2048]{0:T(1024)S(1)} %bitcast.568, f32[2048,96]{1,0:T(8,128)S(1)} %copy.32, f32[]{:T(128)} %constant.1.clone.1), kind=kCustom, calls=%fused_computation.151 | custom fusion | flops 196608 | bytes 393220 | tf_op jit(solution)/shard_map/scatter-add | solution.py:75
  81.6 1.3 collective-permute-start.1
  82.9 5.5 %collective-permute-start = (bf16[1,8,16,96]{3,2,1,0:T(8,128)(2,1)S(1)}, bf16[1,8,16,96]{3,2,1,0:T(8,128)(2,1)S(1)}, u32[]{:S(2)}, u32[]{:S(2)}) collective-permute-start(bf16[1,8,16,96]{3,2,1,0:T(8,128)(2,1)S(1)} %get-tuple-element.71), channel_id=1, source_target_pairs={{0,4},{4,8},{8,12},{12,16},{16,20},{20,24},{24,28},{28,32},{32,36}... | collective-permute-start | bytes 73736 | tf_op jit(solution)/shard_map/ppermute | solution.py:12
  88.6 1.3 collective-permute-start.5
  89.9 5.5 %collective-permute-start.4 = (bf16[1,8,16,96]{3,2,1,0:T(8,128)(2,1)S(1)}, bf16[1,8,16,96]{3,2,1,0:T(8,128)(2,1)S(1)}, u32[]{:S(2)}, u32[]{:S(2)}) collective-permute-start(bf16[1,8,16,96]{3,2,1,0:T(8,128)(2,1)S(1)} %get-tuple-element.67), channel_id=1, source_target_pairs={{0,4},{4,8},{8,12},{12,16},{16,20},{20,24},{24,28},{28,32},{32,36}... | collective-permute-start | bytes 73736 | tf_op jit(solution)/shard_map/ppermute | solution.py:12
  95.4 8.8 %collective-permute-start.3 = (bf16[10,1,16,96]{3,2,1,0:T(8,128)(2,1)S(1)}, bf16[10,1,16,96]{3,2,1,0:T(8,128)(2,1)S(1)}, u32[]{:S(2)}, u32[]{:S(2)}) collective-permute-start(bf16[10,1,16,96]{3,2,1,0:T(8,128)(2,1)S(1)} %get-tuple-element.64), channel_id=1, source_target_pairs={{1,0},{2,1},{3,2},{5,4},{6,5},{7,6},{9,8},{10,9},{11,10},{13,12},{... | collective-permute-start | bytes 92168 | tf_op jit(solution)/shard_map/ppermute | solution.py:15
  104.2 2.1 collective-permute-start.2
  106.4 0.6 pad_maximum_fusion.8
  107.0 2.2 collective-permute-start.7
  109.2 3.5 collective-permute-start.6
  113.3 1.1 fusion.190
  115.3 0.4 fusion.193
  122.1 6.2 %gather_fusion = bf16[2048,96]{1,0:T(8,128)(2,1)S(1)} fusion(bf16[1024,96]{1,0:T(8,128)(2,1)S(1)} %copy.34, s32[2048]{0:T(1024)S(1)} %broadcast_clamp_fusion), kind=kCustom, calls=%fused_computation | custom fusion | bytes 794624 | tf_op jit(solution)/shard_map/gather | solution.py:86
  128.3 1.1 fusion.39
  129.4 0.9 fusion.38
  130.3 14.4 %all-to-all-start.3 = ((bf16[1,1,64,32,96]{4,3,1,0,2:T(8,128)(2,1)}), bf16[1,1,64,32,96]{4,3,1,0,2:T(8,128)(2,1)S(1)}, u32[]{:S(2)}, u32[]{:S(2)}) async-start(bf16[1,1,64,32,96]{4,3,1,0,2:T(8,128)(2,1)} %fusion.39), calls=%async_computation.3 | async-start | bytes 1048576 | tf_op jit(solution)/shard_map/all_to_all | solution.py:91
  145.0 1.1 fusion.189
  146.8 0.9 fusion.19
  147.7 0.9 fusion.37
  148.6 0.9 fusion.36
  149.5 0.9 fusion.18
  150.3 0.9 fusion.35
  151.2 0.9 fusion.34
  152.1 0.9 fusion.17
  153.0 0.9 fusion.33
  153.8 0.9 fusion.32
  154.7 0.9 fusion.16
  155.6 0.9 fusion.31
  156.5 0.9 fusion.30
  157.3 0.9 fusion.29
  158.2 0.9 fusion.28
  159.1 0.9 fusion.27
  159.9 0.9 fusion.15
  160.8 0.9 fusion.26
  161.7 0.9 fusion.25
  162.6 0.9 fusion.14
  163.4 0.9 fusion.24
  164.4 0.4 fusion.191
  170.3 0.9 fusion.23
  171.3 6.2 %gather_fusion.1 = bf16[2048,96]{1,0:T(8,128)(2,1)S(1)} fusion(bf16[1024,96]{1,0:T(8,128)(2,1)S(1)} %copy.36, s32[2048]{0:T(1024)S(1)} %broadcast_clamp_fusion), kind=kCustom, calls=%fused_computation.1 | custom fusion | bytes 794624 | tf_op jit(solution)/shard_map/gather | solution.py:87
  177.5 0.9 fusion.13
  178.4 0.9 fusion.22
  179.3 1.2 fusion
  180.4 11.9 %all-to-all-start.4 = ((bf16[1,1,64,32,128]{4,3,1,0,2:T(8,128)(2,1)}), bf16[1,1,64,32,128]{4,3,1,0,2:T(8,128)(2,1)S(1)}, u32[]{:S(2)}, u32[]{:S(2)}) async-start(bf16[1,1,64,32,128]{4,3,1,0,2:T(8,128)(2,1)} %bitcast.89), calls=%async_computation.4 | async-start | bytes 1048576 | tf_op jit(solution)/shard_map/all_to_all | solution.py:94
  192.4 0.9 fusion.21
  193.3 0.9 fusion.12
  194.2 0.9 fusion.20
  195.1 16.9 %all-to-all-done.4 = bf16[1,1,64,32,128]{4,3,1,0,2:T(8,128)(2,1)S(1)} async-done(((bf16[1,1,64,32,128]{4,3,1,0,2:T(8,128)(2,1)}), bf16[1,1,64,32,128]{4,3,1,0,2:T(8,128)(2,1)S(1)}, u32[]{:S(2)}, u32[]{:S(2)}) %all-to-all-start.4) | async-done | bytes 524320 | tf_op jit(solution)/shard_map/all_to_all | solution.py:94
  211.9 246.7 %all-reduce.4.cloned.1.call-done = f32[27,96,96]{2,1,0:T(8,128)} async-done(((f32[27,96,96]{2,1,0:T(8,128)}), f32[27,96,96]{2,1,0:T(8,128)}) %all-reduce.4.cloned.1.call-update) | async-done | bytes 995344 | tf_op jit(solution)/shard_map/psum | solution.py:84
  458.6 0.8 copy.96
  459.4 0.8 copy.97
  460.2 1.1 copy.98
  (101 shorter events, 16.2 us)
Async XLA Ops:
  7.2 61.9 %copy-start = (bf16[128,96]{0,1:T(8,128)(2,1)S(1)}, bf16[128,96]{0,1:T(8,128)(2,1)}, u32[]{:S(2)}) copy-start(bf16[128,96]{0,1:T(8,128)(2,1)} %param.12) | copy-start | bytes 73732
  8.5 25.9 %all-to-all-start.2 = ((s32[1,1,64]{1,0,2:T(1,128)}), s32[1,1,64]{1,0,2:T(1,128)S(1)}, u32[]{:S(2)}, u32[]{:S(2)}) async-start(s32[1,1,64]{1,0,2:T(1,128)} %copy.31), calls=%async_computation.2 | async-start | bytes 65536 | tf_op jit(solution)/shard_map/all_to_all | solution.py:64
  34.4 15.4 %all-to-all-start = ((s32[1,1,64,32]{3,1,0,2:T(1,128)}), s32[1,1,64,32]{3,1,0,2:T(1,128)S(1)}, u32[]{:S(2)}, u32[]{:S(2)}) async-start(s32[1,1,64,32]{3,1,0,2:T(1,128)} %copy.29), calls=%async_computation | async-start | bytes 65536 | tf_op jit(solution)/shard_map/all_to_all | solution.py:63
  49.8 19.3 %all-to-all-start.1 = ((bf16[1,1,64,32,128]{4,3,1,0,2:T(8,128)(2,1)}), bf16[1,1,64,32,128]{4,3,1,0,2:T(8,128)(2,1)S(1)}, u32[]{:S(2)}, u32[]{:S(2)}) async-start(bf16[1,1,64,32,128]{4,3,1,0,2:T(8,128)(2,1)} %bitcast.566), calls=%async_computation.1 | async-start | bytes 1048576 | tf_op jit(solution)/shard_map/all_to_all | solution.py:62
  69.4 12.0 %copy-start.3 = (bf16[8,8,16,96]{3,2,1,0:T(8,128)(2,1)S(1)}, bf16[8,8,16,96]{3,2,1,0:T(8,128)(2,1)}, u32[]{:S(2)}) copy-start(bf16[8,8,16,96]{3,2,1,0:T(8,128)(2,1)} %param.13) | copy-start | bytes 589828
  81.6 13.8 %collective-permute-start.1 = (bf16[1,8,16,96]{3,2,1,0:T(8,128)(2,1)S(1)}, bf16[1,8,16,96]{3,2,1,0:T(8,128)(2,1)S(1)}, u32[]{:S(2)}, u32[]{:S(2)}) collective-permute-start(bf16[1,8,16,96]{3,2,1,0:T(8,128)(2,1)S(1)} %get-tuple-element.72), channel_id=1, source_target_pairs={{4,0},{8,4},{12,8},{16,12},{20,16},{24,20},{28,24},{32,28},{36,32}... | collective-permute-start | bytes 73736 | tf_op jit(solution)/shard_map/ppermute | solution.py:15
  82.9 12.5 %collective-permute-start = (bf16[1,8,16,96]{3,2,1,0:T(8,128)(2,1)S(1)}, bf16[1,8,16,96]{3,2,1,0:T(8,128)(2,1)S(1)}, u32[]{:S(2)}, u32[]{:S(2)}) collective-permute-start(bf16[1,8,16,96]{3,2,1,0:T(8,128)(2,1)S(1)} %get-tuple-element.71), channel_id=1, source_target_pairs={{0,4},{4,8},{8,12},{12,16},{16,20},{20,24},{24,28},{28,32},{32,36}... | collective-permute-start | bytes 73736 | tf_op jit(solution)/shard_map/ppermute | solution.py:12
  88.6 17.8 %collective-permute-start.5 = (bf16[1,8,16,96]{3,2,1,0:T(8,128)(2,1)S(1)}, bf16[1,8,16,96]{3,2,1,0:T(8,128)(2,1)S(1)}, u32[]{:S(2)}, u32[]{:S(2)}) collective-permute-start(bf16[1,8,16,96]{3,2,1,0:T(8,128)(2,1)S(1)} %get-tuple-element.68), channel_id=1, source_target_pairs={{4,0},{8,4},{12,8},{16,12},{20,16},{24,20},{28,24},{32,28},{36,32}... | collective-permute-start | bytes 73736 | tf_op jit(solution)/shard_map/ppermute | solution.py:15
  89.9 16.5 %collective-permute-start.4 = (bf16[1,8,16,96]{3,2,1,0:T(8,128)(2,1)S(1)}, bf16[1,8,16,96]{3,2,1,0:T(8,128)(2,1)S(1)}, u32[]{:S(2)}, u32[]{:S(2)}) collective-permute-start(bf16[1,8,16,96]{3,2,1,0:T(8,128)(2,1)S(1)} %get-tuple-element.67), channel_id=1, source_target_pairs={{0,4},{4,8},{8,12},{12,16},{16,20},{20,24},{24,28},{28,32},{32,36}... | collective-permute-start | bytes 73736 | tf_op jit(solution)/shard_map/ppermute | solution.py:12
  95.4 17.5 %collective-permute-start.3 = (bf16[10,1,16,96]{3,2,1,0:T(8,128)(2,1)S(1)}, bf16[10,1,16,96]{3,2,1,0:T(8,128)(2,1)S(1)}, u32[]{:S(2)}, u32[]{:S(2)}) collective-permute-start(bf16[10,1,16,96]{3,2,1,0:T(8,128)(2,1)S(1)} %get-tuple-element.64), channel_id=1, source_target_pairs={{1,0},{2,1},{3,2},{5,4},{6,5},{7,6},{9,8},{10,9},{11,10},{13,12},{... | collective-permute-start | bytes 92168 | tf_op jit(solution)/shard_map/ppermute | solution.py:15
  104.2 8.7 %collective-permute-start.2 = (bf16[10,1,16,96]{3,2,1,0:T(8,128)(2,1)S(1)}, bf16[10,1,16,96]{3,2,1,0:T(8,128)(2,1)S(1)}, u32[]{:S(2)}, u32[]{:S(2)}) collective-permute-start(bf16[10,1,16,96]{3,2,1,0:T(8,128)(2,1)S(1)} %get-tuple-element.63), channel_id=1, source_target_pairs={{0,1},{1,2},{2,3},{4,5},{5,6},{6,7},{8,9},{9,10},{10,11},{12,13},{... | collective-permute-start | bytes 92168 | tf_op jit(solution)/shard_map/ppermute | solution.py:12
  107.0 37.7 %collective-permute-start.7 = (bf16[10,1,16,96]{3,2,1,0:T(8,128)(2,1)}, bf16[10,1,16,96]{3,2,1,0:T(8,128)(2,1)S(1)}, u32[]{:S(2)}, u32[]{:S(2)}) collective-permute-start(bf16[10,1,16,96]{3,2,1,0:T(8,128)(2,1)} %get-tuple-element.60), channel_id=1, source_target_pairs={{1,0},{2,1},{3,2},{5,4},{6,5},{7,6},{9,8},{10,9},{11,10},{13,12},{... | collective-permute-start | bytes 92168 | tf_op jit(solution)/shard_map/ppermute | solution.py:15
  109.2 35.5 %collective-permute-start.6 = (bf16[10,1,16,96]{3,2,1,0:T(8,128)(2,1)S(1)}, bf16[10,1,16,96]{3,2,1,0:T(8,128)(2,1)S(1)}, u32[]{:S(2)}, u32[]{:S(2)}) collective-permute-start(bf16[10,1,16,96]{3,2,1,0:T(8,128)(2,1)S(1)} %get-tuple-element.59), channel_id=1, source_target_pairs={{0,1},{1,2},{2,3},{4,5},{5,6},{6,7},{8,9},{9,10},{10,11},{12,13},{... | collective-permute-start | bytes 92168 | tf_op jit(solution)/shard_map/ppermute | solution.py:12
  113.3 1.1 copy-start.1
  130.3 50.1 %all-to-all-start.3 = ((bf16[1,1,64,32,96]{4,3,1,0,2:T(8,128)(2,1)}), bf16[1,1,64,32,96]{4,3,1,0,2:T(8,128)(2,1)S(1)}, u32[]{:S(2)}, u32[]{:S(2)}) async-start(bf16[1,1,64,32,96]{4,3,1,0,2:T(8,128)(2,1)} %fusion.39), calls=%async_computation.3 | async-start | bytes 1048576 | tf_op jit(solution)/shard_map/all_to_all | solution.py:91
  180.4 31.5 %all-to-all-start.4 = ((bf16[1,1,64,32,128]{4,3,1,0,2:T(8,128)(2,1)}), bf16[1,1,64,32,128]{4,3,1,0,2:T(8,128)(2,1)S(1)}, u32[]{:S(2)}, u32[]{:S(2)}) async-start(bf16[1,1,64,32,128]{4,3,1,0,2:T(8,128)(2,1)} %bitcast.89), calls=%async_computation.4 | async-start | bytes 1048576 | tf_op jit(solution)/shard_map/all_to_all | solution.py:94
  192.4 266.2 %all-reduce.4.cloned.1.call-start = ((), (), s32[]{:S(2)}) async-start(), calls=%async_computation.5 | async-start | bytes 2654208 | tf_op jit(solution)/shard_map/psum | solution.py:84
  458.6 1.6 copy-start.2
Sparse Core Ops, SparseCore 0:
  199.2 259.4 all-reduce.3
where the time goes:
time: 469 us; the launch traced here: 468 us
  waiting for transfers between devices  295 us (63%)
  starting transfers between devices  80.9 us (17%)
  matrix products  38.2 us (8%)
  local copies, waits for them, and re-layouts  22.7 us (5%)
  other arithmetic  17.2 us (4%)
  between operations  14.6 us (3%)
    psum x1, waiting for transfers between devices, on_device(): weight_grad = lax.psum(local_grad, ('gx', 'gy'))  247 us
    dot_general x27, matrix products, weight_terms(): lax.dot_general(window, grad_flat, (((0,), (0,)), ((), ())), preferred_el...  23.6 us
    all_to_all x1, waiting for transfers between devices, on_device(): lax.all_to_all(sent_point, 'gx', split_axis=2, concat_axis=2, tiled=True)  16.9 us
    ppermute x4, starting transfers between devices, padded_2(): lax.ppermute(lax.slice_in_dim(block, block.shape[dim] - width, None, axis...  16.6 us
    all_to_all x1, starting transfers between devices, on_device(): lax.all_to_all(counts, 'gx', split_axis=2, concat_axis=2, tiled=True)  15.1 us
    all_to_all x1, starting transfers between devices, on_device(): lax.all_to_all(out_rows.reshape(shape_slots + (width,)), 'gx', split_axis...  14.4 us
    ppermute x4, starting transfers between devices, padded_2(): lax.ppermute(lax.slice_in_dim(block, 0, width, axis=dim), axis, backward)  13.6 us
    all_to_all x1, waiting for transfers between devices, on_device(): lax.all_to_all(points, 'gx', split_axis=2, concat_axis=2, tiled=True)  13.2 us
  transfers between devices with their start and end apart: 14, of which 5 were waited for; matrix products, arithmetic and copies ran while one was open for 13% of the time, Pallas kernels for 0%

commit v1 on v0

v1 whole, which is shorter than its diff:
```python
import functools

import jax
import jax.numpy as jnp
from jax import lax
from jax.experimental import pallas as pl
from jax.experimental.pallas import tpu as pltpu
from jax.sharding import PartitionSpec as P

MESH = pl.DeviceIdType.MESH
F32 = jnp.float32
BF16 = jnp.bfloat16
C = 96
L = 128
CAP = 32
NV = 1024
SUB = 64


def dot(a, b):
    return jnp.dot(a, b, preferred_element_type=F32)


def dot_nt(a, b):
    return lax.dot_general(a, b, (((1,), (1,)), ((), ())), preferred_element_type=F32)


def kernel(
    ngx,
    ngy,
    pz,
    pts,
    vox,
    occ,
    weight,
    w_in,
    cot,
    feat_out,
    grad_out,
    wgrad_out,
    got_pts,
    got_vox,
    rows_d,
    rows_y,
    got_d,
    got_y,
    gpad,
    fpad,
    wf,
    wb,
    winp,
    wint,
    oht,
    field_d,
    field_y,
    wg,
    pk,
    rs_buf,
    z_buf,
    ag_buf,
    vox_s,
    vox_r,
    pts_s,
    pts_r,
    d_s,
    d_r,
    y_s,
    y_r,
    rs_s,
    rs_r,
    z_s,
    z_r,
    ag_s,
    ag_r,
    g_s,
    g_r,
    f_s,
    f_r,
):
    gx = lax.axis_index("gx")
    gy = lax.axis_index("gy")
    nz = ngx // pz
    plane = pz * ngy
    zi = gx // pz
    xy = lax.rem(gx, pz)
    slot = xy * ngy + gy
    rows = ngx * CAP

    gpad[...] = jnp.zeros_like(gpad)
    fpad[...] = jnp.zeros_like(fpad)

    barrier = pltpu.get_barrier_semaphore()

    def greet(px, py):
        pl.semaphore_signal(barrier, inc=1, device_id=(px, py), device_id_type=MESH)

    @pl.loop(1, ngx)
    def _(k):
        greet(lax.rem(gx + k, ngx), gy)

    @pl.loop(0, pz)
    def _(k):
        for m in range(1, ngy):
            greet(zi * pz + k, lax.rem(gy + m, ngy))

    directions = ((1, 0), (-1, 0), (0, 1), (0, -1), (1, 1), (1, -1), (-1, 1), (-1, -1))

    def exists(dx, dy):
        ok = jnp.bool_(True)
        if dx == 1:
            ok = ok & (gx < ngx - 1)
        if dx == -1:
            ok = ok & (gx > 0)
        if dy == 1:
            ok = ok & (gy < ngy - 1)
        if dy == -1:
            ok = ok & (gy > 0)
        return ok

    for dx, dy in directions[4:]:

        @pl.when(exists(dx, dy))
        def _():
            greet(gx + dx, gy + dy)

    o0 = occ[0].astype(F32)
    o1 = occ[1].astype(F32)

    @pl.loop(0, 8)
    def _(x):
        value = cot[x].astype(F32)
        z = lax.broadcasted_iota(jnp.int32, value.shape, 1)
        gpad[x + 1, pl.ds(1, 8), :, pl.ds(0, C)] = (value * jnp.where(z < 8, o0, o1)).astype(BF16)

    wf[...] = jnp.zeros_like(wf)
    wb[...] = jnp.zeros_like(wb)
    for tap in range(27):
        ab, c = tap // 3, tap % 3
        value = weight[tap]
        wf[ab * L : ab * L + C, c * L : c * L + C] = value
        wb[c * L : c * L + C, ab * L : ab * L + C] = value
    winp[...] = jnp.zeros_like(winp)
    winp[:, 0:C] = w_in[...]
    wint[...] = jnp.transpose(winp[...].astype(F32)).astype(BF16)

    corners = sum(
        (exists(dx, dy).astype(jnp.int32) for dx, dy in directions[4:]), jnp.int32(0)
    )
    pl.semaphore_wait(barrier, (ngx - 1) + pz * (ngy - 1) + corners)

    def exchange(src, dst, send, recv):
        @pl.loop(1, ngx)
        def _(k):
            peer = lax.rem(gx + k, ngx)
            pltpu.make_async_remote_copy(
                src_ref=src.at[peer],
                dst_ref=dst.at[gx],
                send_sem=send,
                recv_sem=recv,
                device_id=(peer, gy),
                device_id_type=MESH,
            ).start()

    def whole(ref, count, send, recv):
        part = ref.at[pl.ds(0, count)]
        return pltpu.make_async_remote_copy(
            src_ref=part,
            dst_ref=part,
            send_sem=send,
            recv_sem=recv,
            device_id=(gx, gy),
            device_id_type=MESH,
        )

    def halo(ref, d, send, recv):
        dx, dy = directions[d]

        def span(delta, edge):
            if delta == 0:
                return pl.ds(1, 8), pl.ds(1, 8)
            return (8, 0) if delta == 1 else (1, 9)

        sx, tx = span(dx, 0)
        sy, ty = span(dy, 0)
        return pltpu.make_async_remote_copy(
            src_ref=ref.at[sx, sy],
            dst_ref=ref.at[tx, ty],
            send_sem=send.at[d],
            recv_sem=recv.at[d],
            device_id=(gx + dx, gy + dy),
            device_id_type=MESH,
        )

    def halo_start(ref, send, recv):
        for d, (dx, dy) in enumerate(directions):

            @pl.when(exists(dx, dy))
            def _():
                halo(ref, d, send, recv).start()

    def halo_wait(ref, send, recv):
        for d, (dx, dy) in enumerate(directions):

            @pl.when(exists(-dx, -dy))
            def _():
                halo(ref, d, send, recv).wait_recv()

    def halo_sent(ref, send, recv):
        for d, (dx, dy) in enumerate(directions):

            @pl.when(exists(dx, dy))
            def _():
                halo(ref, d, send, recv).wait_send()

    exchange(vox, got_vox, vox_s, vox_r)
    halo_start(gpad, g_s, g_r)
    exchange(pts, got_pts, pts_s, pts_r)
    got_vox[gx] = vox[gx]
    got_pts[gx] = pts[gx]

    def lift(total, lower, upper):
        count = total.shape[0]
        z = lax.broadcasted_iota(jnp.int32, total.shape, 0) % 16
        down = pltpu.roll(lower, 1, 0)
        up = pltpu.roll(upper, count - 1, 0)
        total = total + jnp.where(z == 0, 0.0, down) + jnp.where(z == 15, 0.0, up)
        return total * jnp.where(z < 8, o0, o1)

    step = 4

    halo_wait(gpad, g_s, g_r)

    @pl.loop(0, 8 // step)
    def _(i):
        windows = [
            gpad[pl.ds(i * step + 2 - a, step), 2 - b : 10 - b].reshape(step * L, L)
            for a in range(3)
            for b in range(3)
        ]
        z3 = dot_nt(jnp.concatenate(windows, axis=1), wb[...])
        out = lift(z3[:, L : 2 * L], z3[:, 2 * L :], z3[:, :L])
        field_d[pl.ds(pl.multiple_of(i * step * L, step * L), step * L), :] = out.astype(BF16)

    whole(got_vox, ngx - 1, vox_s, vox_r).wait_recv()
    chunk = min(256, rows)
    ids = got_vox[...].reshape(ngx, L)
    high = (ids >> 5).astype(F32).astype(BF16)
    low = (ids & 31).astype(F32).astype(BF16)
    ones = jnp.ones((L, L), BF16)

    @pl.loop(0, rows // chunk)
    def _(i):
        owner = lax.broadcasted_iota(jnp.int32, (chunk, ngx), 0) // CAP + i * (chunk // CAP)
        pick = jnp.where(
            owner == lax.broadcasted_iota(jnp.int32, (chunk, ngx), 1), 1.0, 0.0
        ).astype(BF16)
        here = (
            lax.broadcasted_iota(jnp.int32, (chunk, L), 0) % CAP
            == lax.broadcasted_iota(jnp.int32, (chunk, L), 1)
        )
        hi = jnp.where(here, dot(pick, high) * 32.0, 0.0).astype(BF16)
        lo = jnp.where(here, dot(pick, low), 0.0).astype(BF16)
        wanted = dot(hi, ones) + dot(lo, ones)
        lane = lax.broadcasted_iota(jnp.int32, (chunk, L), 1).astype(F32)
        for j in range(NV // L):
            oht[pl.ds(pl.multiple_of(i * chunk, chunk), chunk), j * L : (j + 1) * L] = jnp.where(
                wanted == lane + float(j * L), 1.0, 0.0
            ).astype(BF16)

    group = min(512, rows)

    def gather(field, out):
        @pl.loop(0, rows // group)
        def _(i):
            got = dot(oht[pl.ds(pl.multiple_of(i * group, group), group), :], field[...])
            out[pl.ds(i * (group // CAP), group // CAP)] = got.astype(BF16).reshape(
                group // CAP, CAP, L
            )

    gather(field_d, rows_d)
    exchange(rows_d, got_d, d_s, d_r)
    got_d[gx] = rows_d[gx]

    whole(got_pts, ngx - 1, pts_s, pts_r).wait_recv()
    proj_t = dot_nt(wint[...], got_pts[...].reshape(rows, L)).astype(BF16)
    sum_t = dot(proj_t, oht[...])
    z_lane = lax.broadcasted_iota(jnp.int32, sum_t.shape, 1) % 16
    sum_t = (sum_t * jnp.where(z_lane < 8, o0, o1)).astype(BF16).astype(F32)
    f0 = jnp.transpose(sum_t).astype(BF16).reshape(8, 8, 16, L)
    fpad[1:9, 1:9] = f0
    halo_start(fpad, f_s, f_r)

    f_t = sum_t[:C]
    z_own = z_lane[:C]
    stack = jnp.concatenate(
        [
            jnp.where(z_own == 0, 0.0, pltpu.roll(f_t, 1, 1)),
            f_t,
            jnp.where(z_own == 15, 0.0, pltpu.roll(f_t, NV - 1, 1)),
        ],
        axis=0,
    ).astype(BF16)
    for ab in range(9):
        a, b = ab // 3, ab % 3
        window = gpad[2 - a : 10 - a, 2 - b : 10 - b].reshape(NV, L)
        wg[:, ab * L : (ab + 1) * L] = dot(stack, window)

    def tap_block(tap):
        ab, c = tap // 3, tap % 3
        return wg[c * C : (c + 1) * C, ab * L : (ab + 1) * L]

    lane = lax.broadcasted_iota(jnp.int32, (C, L), 1)
    for g in range(7):
        last = tap_block(4 * g + 3) if g < 6 else jnp.zeros((C, L), F32)
        for j in range(3):
            extra = pltpu.roll(last, C - 32 * j, 1)
            block = jnp.where(lane < C, tap_block(4 * g + j), extra)
            pk[9 * g + 3 * j : 9 * g + 3 * j + 3] = block.astype(BF16).reshape(3, CAP, L)
    pk[63] = jnp.zeros((CAP, L), BF16)

    sub = SUB // plane

    @pl.loop(1, plane)
    def _(k):
        peer = lax.rem(slot + k, plane)
        pltpu.make_async_remote_copy(
            src_ref=pk.at[pl.ds(peer * sub, sub)],
            dst_ref=rs_buf.at[slot],
            send_sem=rs_s,
            recv_sem=rs_r,
            device_id=(zi * pz + peer // ngy, lax.rem(peer, ngy)),
            device_id_type=MESH,
        ).start()

    rs_buf[slot] = pk[pl.ds(slot * sub, sub)]

    halo_wait(fpad, f_s, f_r)

    @pl.loop(0, 8 // step)
    def _(i):
        windows = [
            fpad[pl.ds(i * step + a, step), b : b + 8].reshape(step * L, L)
            for a in range(3)
            for b in range(3)
        ]
        z3 = dot(jnp.concatenate(windows, axis=1), wf[...])
        out = lift(z3[:, L : 2 * L], z3[:, :L], z3[:, 2 * L :])
        field_y[pl.ds(pl.multiple_of(i * step * L, step * L), step * L), :] = out.astype(BF16)

    gather(field_y, rows_y)
    exchange(rows_y, got_y, y_s, y_r)
    got_y[gx] = rows_y[gx]

    whole(rs_buf, plane - 1, rs_s, rs_r).wait_recv()
    total = rs_buf[0].astype(F32)
    for k in range(1, plane):
        total = total + rs_buf[k].astype(F32)
    z_buf[zi] = total.astype(BF16)

    @pl.loop(1, nz)
    def _(k):
        peer = lax.rem(zi + k, nz)
        pltpu.make_async_remote_copy(
            src_ref=z_buf.at[zi],
            dst_ref=z_buf.at[zi],
            send_sem=z_s,
            recv_sem=z_r,
            device_id=(peer * pz + xy, gy),
            device_id_type=MESH,
        ).start()

    whole(got_d, ngx - 1, d_s, d_r).wait_recv()

    @pl.loop(0, rows // group)
    def _(i):
        part = pl.ds(i * (group // CAP), group // CAP)
        got = dot_nt(got_d[part].reshape(group, L), winp[...])
        grad_out[part] = got.astype(BF16).reshape(group // CAP, CAP, L)

    whole(z_buf, nz - 1, z_s, z_r).wait_recv()
    total = z_buf[0].astype(F32)
    for k in range(1, nz):
        total = total + z_buf[k].astype(F32)
    ag_buf[slot] = total.astype(BF16)

    @pl.loop(1, plane)
    def _(k):
        peer = lax.rem(slot + k, plane)
        pltpu.make_async_remote_copy(
            src_ref=ag_buf.at[slot],
            dst_ref=ag_buf.at[slot],
            send_sem=ag_s,
            recv_sem=ag_r,
            device_id=(zi * pz + peer // ngy, lax.rem(peer, ngy)),
            device_id_type=MESH,
        ).start()

    whole(got_y, ngx - 1, y_s, y_r).wait_recv()
    feat_out[...] = got_y[:, :, 0:C]

    whole(ag_buf, plane - 1, ag_s, ag_r).wait_recv()
    summed = ag_buf[...].reshape(SUB, CAP, L)
    for g in range(7):
        blocks = [
            summed[9 * g + 3 * j : 9 * g + 3 * j + 3].reshape(C, L).astype(F32) for j in range(3)
        ]
        for j in range(3):
            wgrad_out[4 * g + j] = blocks[j][:, :C]
        if g < 6:
            last = pltpu.roll(blocks[0], 32, 1)
            for j in (1, 2):
                moved = pltpu.roll(blocks[j], 32 + 32 * j, 1)
                last = jnp.where(lane >= 32 * j, moved, last)
            wgrad_out[4 * g + 3] = last[:, :C]

    whole(vox, ngx - 1, vox_s, vox_r).wait_send()
    whole(pts, ngx - 1, pts_s, pts_r).wait_send()
    whole(rows_d, ngx - 1, d_s, d_r).wait_send()
    whole(rows_y, ngx - 1, y_s, y_r).wait_send()
    whole(rs_buf, plane - 1, rs_s, rs_r).wait_send()
    whole(z_buf, nz - 1, z_s, z_r).wait_send()
    whole(ag_buf, plane - 1, ag_s, ag_r).wait_send()
    halo_sent(gpad, g_s, g_r)
    halo_sent(fpad, f_s, f_r)


def on_device(ngx, ngy, pz, points, counts, voxels, occupancy, weight, w_in, cotangent):
    slots = lax.broadcasted_iota(jnp.int32, (ngx, CAP), 1)
    used = jnp.where(slots < counts[0, 0][:, None], voxels[0, 0], -32)
    used = jnp.pad(used, ((0, 0), (0, L - CAP))).reshape(ngx, 1, L)
    rows = ngx * CAP
    nz = ngx // pz
    plane = pz * ngy
    vmem = pl.BlockSpec(memory_space=pltpu.VMEM)
    dma = pltpu.SemaphoreType.DMA
    feat, grad, wgrad = pl.pallas_call(
        functools.partial(kernel, ngx, ngy, pz),
        out_shape=(
            jax.ShapeDtypeStruct((ngx, CAP, C), BF16),
            jax.ShapeDtypeStruct((ngx, CAP, L), BF16),
            jax.ShapeDtypeStruct((27, C, C), F32),
        ),
        in_specs=[vmem, vmem, pl.BlockSpec(memory_space=pltpu.SMEM), vmem, vmem, vmem],
        out_specs=(vmem, vmem, vmem),
        scratch_shapes=[
            pltpu.VMEM((ngx, CAP, L), BF16),
            pltpu.VMEM((ngx, 1, L), jnp.int32),
            pltpu.VMEM((ngx, CAP, L), BF16),
            pltpu.VMEM((ngx, CAP, L), BF16),
            pltpu.VMEM((ngx, CAP, L), BF16),
            pltpu.VMEM((ngx, CAP, L), BF16),
            pltpu.VMEM((10, 10, 16, L), BF16),
            pltpu.VMEM((10, 10, 16, L), BF16),
            pltpu.VMEM((9 * L, 3 * L), BF16),
            pltpu.VMEM((3 * L, 9 * L), BF16),
            pltpu.VMEM((L, L), BF16),
            pltpu.VMEM((L, L), BF16),
            pltpu.VMEM((rows, NV), BF16),
            pltpu.VMEM((NV, L), BF16),
            pltpu.VMEM((NV, L), BF16),
            pltpu.VMEM((3 * C, 9 * L), F32),
            pltpu.VMEM((SUB, CAP, L), BF16),
            pltpu.VMEM((plane, SUB // plane, CAP, L), BF16),
            pltpu.VMEM((nz, SUB // plane, CAP, L), BF16),
            pltpu.VMEM((plane, SUB // plane, CAP, L), BF16),
        ]
        + [dma] * 14
        + [dma((8,))] * 4,
        compiler_params=pltpu.CompilerParams(
            collective_id=0, has_side_effects=True, vmem_limit_bytes=56 * 1024 * 1024
        ),
    )(
        points.reshape(ngx, CAP, L),
        used,
        occupancy.reshape(2),
        weight,
        w_in,
        cotangent,
    )
    return feat[None, None], grad[None, None], wgrad


def solution(mesh):
    ngx, ngy = mesh.shape["gx"], mesh.shape["gy"]
    pz = ngx // 8
    placed = (
        P("gy", "gx", None, None, None),
        P("gy", "gx", None),
        P("gy", "gx", None, None),
        P("gx", "gy", None),
        P(),
        P(),
        P("gx", "gy", None, None),
    )
    return jax.shard_map(
        functools.partial(on_device, ngx, ngy, pz),
        mesh=mesh,
        in_specs=placed,
        out_specs=(P("gy", "gx", None, None, None), P("gy", "gx", None, None, None), P()),
        check_vma=False,
    )
```

time: 469 us -> 83.4 us (0.18)
  waiting for transfers between devices: 295 us -> 0 us
  starting transfers between devices: 80.9 us -> 0 us
  Pallas kernels: 0 us -> 73.9 us
  matrix products: 38.2 us -> 0 us
  other arithmetic: 17.2 us -> 0.73 us
  local copies, waits for them, and re-layouts: 22.7 us -> 7.78 us
  between operations: 14.6 us -> 0.65 us
    psum x1 -> x0, waiting for transfers between devices: 247 us -> none  [on_device(): weight_grad = lax.psum(local_grad, ('gx', 'gy'))]
    pallas_call x0 -> x1, Pallas kernels: none -> 73.9 us  [on_device(): pl.pallas_call(functools.partial(kernel, ngx, ngy, pz), out_shape=(jax.Sh...]
    all_to_all x5 -> x0, starting transfers between devices: 50.7 us -> none  [the longest x1 15.1 us: on_device(): lax.all_to_all(counts, 'gx', split_axis=2, concat_axis=2, tiled=True)]
    all_to_all x5 -> x0, waiting for transfers between devices: 47.9 us -> none  [the longest x1 16.9 us: on_device(): lax.all_to_all(sent_point, 'gx', split_axis=2, concat_axis=2, tiled=True)]
    dot_general x83 -> x0, matrix products: 38.2 us -> none  [the longest x27 23.6 us: weight_terms(): lax.dot_general(window, grad_flat, (((0,), (0,)), ((), ())), preferred_el...]
    ppermute x8 -> x0, starting transfers between devices: 30.2 us -> none  [the longest x4 16.6 us: padded_2(): lax.ppermute(lax.slice_in_dim(block, block.shape[dim] - width, None, axis...]
    gather x2 -> x0, local copies, waits for them, and re-layouts: 12.4 us -> none  [the longest x1 6.18 us: on_device(): grad_rows = feature_grad[flat_index]]
    scatter-add x1 -> x0, other arithmetic: 11.6 us -> none  [on_device(): jnp.zeros((64 * depth, width), jnp.float32).at[flat_index]]
  transfers between devices with their start and end apart: 14 -> 0, of which waited for: 5 -> 0; matrix products, arithmetic and copies ran while one was open for 13% -> 0% of each run, Pallas kernels for 0% -> 0%
where the time goes in v1:
time: 83.4 us; the launch traced here: 83.1 us
  Pallas kernels  73.9 us (89%)
  local copies, waits for them, and re-layouts  7.78 us (9%)
    pallas_call x1, Pallas kernels, on_device(): pl.pallas_call(functools.partial(kernel, ngx, ngy, pz), out_shape=(jax.Sh...  73.9 us
    unnamed x7, local copies, waits for them, and re-layouts  7.15 us

profile of v1, /device:TPU:1, one launch (start us, length us, event | category | flops | bytes accessed | tf_op | source)
XLA Modules:
  0.0 83.1 jit_solution(17012709489132844829)
XLA Ops:
  0.6 0.8 copy.10
  1.4 0.7 bitcast_select_fusion
  2.2 0.6 pad.4
  2.8 1.5 %copy.11.w_in = bf16[128,96]{1,0:T(8,128)(2,1)} copy(bf16[128,96]{0,1:T(8,128)(2,1)} %param.12) | data formatting | bytes 49152 | tf_op args[5]
  4.2 73.9 %shard_map.94 = (bf16[64,32,96]{2,1,0:T(8,128)(2,1)}, bf16[64,32,128]{2,1,0:T(8,128)(2,1)}, f32[27,96,96]{2,1,0:T(8,128)}) custom-call(bf16[64,32,128]{2,1,0:T(8,128)(2,1)} %bitcast.8, s32[64,1,128]{2,1,0:T(1,128)} %bitcast.11, s32[2]{0:T(128)} %bitcast.13, bf16[27,96,96]{2,1,0:T(8,128)(2,1)} %weight.1, bf16[128,96]{1,0:T(8,128)(2,1)} %copy.11.w_in, ...), custom_call_target="tpu_custom_call" | custom-call | tf_op jit(solution)/shard_map/pallas_call | solution.py:436
  78.2 0.0 copy-start
  78.2 2.0 %copy.15 = bf16[1,1,64,32,96]{4,3,2,1,0:T(8,128)(2,1)} copy(bf16[1,1,64,32,96]{4,3,2,1,0:T(8,128)(2,1)} %bitcast.10) | data formatting | bytes 786432
  80.2 1.9 %copy.16 = bf16[1,1,64,32,128]{4,3,2,1,0:T(8,128)(2,1)} copy(bf16[1,1,64,32,128]{4,3,2,1,0:T(8,128)(2,1)} %bitcast.9) | data formatting | bytes 1048576
  82.0 0.0 copy-done
  82.0 1.1 %copy.17 = f32[27,96,96]{2,1,0:T(8,128)} copy(f32[27,96,96]{2,1,0:T(8,128)S(1)} %copy-done) | data formatting | bytes 1990656
Async XLA Ops:
  78.2 3.9 %copy-start = (f32[27,96,96]{2,1,0:T(8,128)S(1)}, f32[27,96,96]{2,1,0:T(8,128)}, u32[]{:S(2)}) copy-start(f32[27,96,96]{2,1,0:T(8,128)} %get-tuple-element.14) | copy-start | bytes 2985988

commit v2 on v1

--- a/solution.py
+++ b/solution.py
@@ -15,6 +15,7 @@
 CAP = 32
 NV = 1024
 SUB = 64
+PACK = CAP * C // L
 
 
 def dot(a, b):
@@ -23,6 +24,33 @@
 
 def dot_nt(a, b):
     return lax.dot_general(a, b, (((1,), (1,)), ((), ())), preferred_element_type=F32)
+
+
+def pack(value, owners):
+    tiles = value.reshape(owners, 4, 8, L)
+    tail = tiles[:, 3].reshape(owners * 8, L)
+    lane = lax.broadcasted_iota(jnp.int32, (owners * 8, L), 1)
+    parts = [
+        jnp.where(
+            lane < C, tiles[:, j].reshape(owners * 8, L), pltpu.roll(tail, C - 32 * j, 1)
+        ).reshape(owners, 1, 8, L)
+        for j in range(3)
+    ]
+    return jnp.concatenate(parts, axis=1).reshape(owners, PACK, L)
+
+
+def unpack(value, owners):
+    tiles = value.reshape(owners, 3, 8, L)
+    lane = lax.broadcasted_iota(jnp.int32, (owners * 8, L), 1)
+    parts = [tiles[:, j].reshape(owners * 8, L) for j in range(3)]
+    tail = jnp.zeros((owners * 8, L), value.dtype)
+    for j in range(3):
+        moved = pltpu.roll(parts[j], 32 + 32 * j, 1)
+        tail = jnp.where((lane >= 32 * j) & (lane < 32 * j + 32), moved, tail)
+    parts = [jnp.where(lane < C, part, 0.0) for part in parts] + [tail]
+    return jnp.concatenate([part.reshape(owners, 1, 8, L) for part in parts], axis=1).reshape(
+        owners * CAP, L
+    )
 
 
 def kernel(
@@ -30,25 +58,26 @@
     ngy,
     pz,
     pts,
-    vox,
+    voxels_t,
+    counts,
     occ,
     weight,
-    w_in,
+    w_in_t,
     cot,
-    feat_out,
-    grad_out,
-    wgrad_out,
-    got_pts,
+    got_y,
+    got_d,
+    ag_buf,
+    vox,
+    rows_p,
+    got_p,
+    proj,
     got_vox,
     rows_d,
     rows_y,
-    got_d,
-    got_y,
     gpad,
     fpad,
     wf,
     wb,
-    winp,
     wint,
     oht,
     field_d,
@@ -57,7 +86,6 @@
     pk,
     rs_buf,
     z_buf,
-    ag_buf,
     vox_s,
     vox_r,
     pts_s,
@@ -123,6 +151,14 @@
         def _():
             greet(gx + dx, gy + dy)
 
+    used = jnp.where(
+        lax.broadcasted_iota(jnp.int32, (CAP, ngx), 0) < counts[...], voxels_t[...], -32
+    ).astype(F32)
+    used = jnp.concatenate([used, jnp.zeros((L - CAP, ngx), F32)], axis=0)
+    if ngx < L:
+        used = jnp.concatenate([used, jnp.zeros((L, L - ngx), F32)], axis=1)
+    vox[...] = jnp.transpose(used)[:ngx].astype(jnp.int32).reshape(ngx, 1, L)
+
     o0 = occ[0].astype(F32)
     o1 = occ[1].astype(F32)
 
@@ -139,9 +175,18 @@
         value = weight[tap]
         wf[ab * L : ab * L + C, c * L : c * L + C] = value
         wb[c * L : c * L + C, ab * L : ab * L + C] = value
-    winp[...] = jnp.zeros_like(winp)
-    winp[:, 0:C] = w_in[...]
-    wint[...] = jnp.transpose(winp[...].astype(F32)).astype(BF16)
+    wint[...] = jnp.zeros_like(wint)
+    wint[0:C, :] = w_in_t[...]
+
+    group = min(512, rows)
+    own = group // CAP
+
+    @pl.loop(0, rows // group)
+    def _(i):
+        part = pl.ds(i * own, own)
+        value = dot_nt(pts[part].reshape(group, L), wint[...])
+        rows_p[part] = pack(value, own).astype(BF16)
+
 
     corners = sum(
         (exists(dx, dy).astype(jnp.int32) for dx, dy in directions[4:]), jnp.int32(0)
@@ -214,9 +259,9 @@
 
     exchange(vox, got_vox, vox_s, vox_r)
     halo_start(gpad, g_s, g_r)
-    exchange(pts, got_pts, pts_s, pts_r)
+    exchange(rows_p, got_p, pts_s, pts_r)
     got_vox[gx] = vox[gx]
-    got_pts[gx] = pts[gx]
+    got_p[gx] = rows_p[gx]
 
     def lift(total, lower, upper):
         count = total.shape[0]
@@ -267,22 +312,27 @@
                 wanted == lane + float(j * L), 1.0, 0.0
             ).astype(BF16)
 
-    group = min(512, rows)
-
     def gather(field, out):
         @pl.loop(0, rows // group)
         def _(i):
             got = dot(oht[pl.ds(pl.multiple_of(i * group, group), group), :], field[...])
-            out[pl.ds(i * (group // CAP), group // CAP)] = got.astype(BF16).reshape(
-                group // CAP, CAP, L
-            )
+            out[pl.ds(i * own, own)] = pack(got, own).astype(BF16)
 
     gather(field_d, rows_d)
-    exchange(rows_d, got_d, d_s, d_r)
-    got_d[gx] = rows_d[gx]
-
-    whole(got_pts, ngx - 1, pts_s, pts_r).wait_recv()
-    proj_t = dot_nt(wint[...], got_pts[...].reshape(rows, L)).astype(BF16)
+
+    whole(got_p, ngx - 1, pts_s, pts_r).wait_recv()
+
+    @pl.loop(0, rows // group)
+    def _(i):
+        value = unpack(got_p[pl.ds(i * own, own)].astype(F32), own)
+        proj[pl.ds(pl.multiple_of(i * group, group), group), :] = value.astype(BF16)
+
+    eye = jnp.where(
+        lax.broadcasted_iota(jnp.int32, (L, L), 0) == lax.broadcasted_iota(jnp.int32, (L, L), 1),
+        1.0,
+        0.0,
+    ).astype(BF16)
+    proj_t = dot_nt(eye, proj[...]).astype(BF16)
     sum_t = dot(proj_t, oht[...])
     z_lane = lax.broadcasted_iota(jnp.int32, sum_t.shape, 1) % 16
     sum_t = (sum_t * jnp.where(z_lane < 8, o0, o1)).astype(BF16).astype(F32)
@@ -333,6 +383,8 @@
         ).start()
 
     rs_buf[slot] = pk[pl.ds(slot * sub, sub)]
+    exchange(rows_d, got_d, d_s, d_r)
+    got_d[gx] = rows_d[gx]
 
     halo_wait(fpad, f_s, f_r)
 
@@ -369,14 +421,6 @@
             device_id_type=MESH,
         ).start()
 
-    whole(got_d, ngx - 1, d_s, d_r).wait_recv()
-
-    @pl.loop(0, rows // group)
-    def _(i):
-        part = pl.ds(i * (group // CAP), group // CAP)
-        got = dot_nt(got_d[part].reshape(group, L), winp[...])
-        grad_out[part] = got.astype(BF16).reshape(group // CAP, CAP, L)
-
     whole(z_buf, nz - 1, z_s, z_r).wait_recv()
     total = z_buf[0].astype(F32)
     for k in range(1, nz):
@@ -395,26 +439,12 @@
             device_id_type=MESH,
         ).start()
 
+    whole(got_d, ngx - 1, d_s, d_r).wait_recv()
     whole(got_y, ngx - 1, y_s, y_r).wait_recv()
-    feat_out[...] = got_y[:, :, 0:C]
-
     whole(ag_buf, plane - 1, ag_s, ag_r).wait_recv()
-    summed = ag_buf[...].reshape(SUB, CAP, L)
-    for g in range(7):
-        blocks = [
-            summed[9 * g + 3 * j : 9 * g + 3 * j + 3].reshape(C, L).astype(F32) for j in range(3)
-        ]
-        for j in range(3):
-            wgrad_out[4 * g + j] = blocks[j][:, :C]
-        if g < 6:
-            last = pltpu.roll(blocks[0], 32, 1)
-            for j in (1, 2):
-                moved = pltpu.roll(blocks[j], 32 + 32 * j, 1)
-                last = jnp.where(lane >= 32 * j, moved, last)
-            wgrad_out[4 * g + 3] = last[:, :C]
 
     whole(vox, ngx - 1, vox_s, vox_r).wait_send()
-    whole(pts, ngx - 1, pts_s, pts_r).wait_send()
+    whole(rows_p, ngx - 1, pts_s, pts_r).wait_send()
     whole(rows_d, ngx - 1, d_s, d_r).wait_send()
     whole(rows_y, ngx - 1, y_s, y_r).wait_send()
     whole(rs_buf, plane - 1, rs_s, rs_r).wait_send()
@@ -424,36 +454,59 @@
     halo_sent(fpad, f_s, f_r)
 
 
+def finish(own, got_y, got_d, summed, w_in_t, feat_out, grad_out, wgrad_out):
+    step = pl.program_id(0)
+    part = pl.ds(jnp.minimum(step, got_y.shape[0] // own - 1) * own, own)
+    feat = unpack(got_y[part].astype(F32), own).astype(BF16)
+    feat_out[...] = feat[:, :C].reshape(own, CAP, C)
+    grad = unpack(got_d[part].astype(F32), own)[:, :C].astype(BF16)
+    grad_out[...] = dot(grad, w_in_t[...]).astype(BF16).reshape(own, CAP, L)
+
+    lane = lax.broadcasted_iota(jnp.int32, (C, L), 1)
+    first = 9 * jnp.minimum(step, 6)
+    sub = summed.shape[1]
+    blocks = [
+        jnp.concatenate(
+            [summed[(first + r) // sub, lax.rem(first + r, sub)] for r in range(3 * j, 3 * j + 3)]
+        ).astype(F32)
+        for j in range(3)
+    ]
+    for j in range(3):
+        wgrad_out[j] = blocks[j][:, :C]
+    last = pltpu.roll(blocks[0], 32, 1)
+    for j in (1, 2):
+        moved = pltpu.roll(blocks[j], 32 + 32 * j, 1)
+        last = jnp.where(lane >= 32 * j, moved, last)
+    wgrad_out[3] = last[:, :C]
+
+
 def on_device(ngx, ngy, pz, points, counts, voxels, occupancy, weight, w_in, cotangent):
-    slots = lax.broadcasted_iota(jnp.int32, (ngx, CAP), 1)
-    used = jnp.where(slots < counts[0, 0][:, None], voxels[0, 0], -32)
-    used = jnp.pad(used, ((0, 0), (0, L - CAP))).reshape(ngx, 1, L)
     rows = ngx * CAP
     nz = ngx // pz
     plane = pz * ngy
     vmem = pl.BlockSpec(memory_space=pltpu.VMEM)
     dma = pltpu.SemaphoreType.DMA
-    feat, grad, wgrad = pl.pallas_call(
+    got_y, got_d, summed = pl.pallas_call(
         functools.partial(kernel, ngx, ngy, pz),
         out_shape=(
-            jax.ShapeDtypeStruct((ngx, CAP, C), BF16),
-            jax.ShapeDtypeStruct((ngx, CAP, L), BF16),
-            jax.ShapeDtypeStruct((27, C, C), F32),
+            pltpu.VMEM((ngx, PACK, L), BF16),
+            pltpu.VMEM((ngx, PACK, L), BF16),
+            pltpu.VMEM((plane, SUB // plane, CAP, L), BF16),
         ),
-        in_specs=[vmem, vmem, pl.BlockSpec(memory_space=pltpu.SMEM), vmem, vmem, vmem],
+        in_specs=[vmem, vmem, vmem, pl.BlockSpec(memory_space=pltpu.SMEM), vmem, vmem, vmem],
         out_specs=(vmem, vmem, vmem),
         scratch_shapes=[
-            pltpu.VMEM((ngx, CAP, L), BF16),
             pltpu.VMEM((ngx, 1, L), jnp.int32),
-            pltpu.VMEM((ngx, CAP, L), BF16),
-            pltpu.VMEM((ngx, CAP, L), BF16),
-            pltpu.VMEM((ngx, CAP, L), BF16),
-            pltpu.VMEM((ngx, CAP, L), BF16),
+            pltpu.VMEM((ngx, PACK, L), BF16),
+            pltpu.VMEM((ngx, PACK, L), BF16),
+            pltpu.VMEM((rows, L), BF16),
+            pltpu.VMEM((ngx, 1, L), jnp.int32),
+            pltpu.VMEM((ngx, PACK, L), BF16),
+            pltpu.VMEM((ngx, PACK, L), BF16),
             pltpu.VMEM((10, 10, 16, L), BF16),
             pltpu.VMEM((10, 10, 16, L), BF16),
             pltpu.VMEM((9 * L, 3 * L), BF16),
             pltpu.VMEM((3 * L, 9 * L), BF16),
-            pltpu.VMEM((L, L), BF16),
             pltpu.VMEM((L, L), BF16),
             pltpu.VMEM((rows, NV), BF16),
             pltpu.VMEM((NV, L), BF16),
@@ -462,7 +515,6 @@
             pltpu.VMEM((SUB, CAP, L), BF16),
             pltpu.VMEM((plane, SUB // plane, CAP, L), BF16),
             pltpu.VMEM((nz, SUB // plane, CAP, L), BF16),
-            pltpu.VMEM((plane, SUB // plane, CAP, L), BF16),
         ]
         + [dma] * 14
         + [dma((8,))] * 4,
@@ -471,11 +523,33 @@
         ),
     )(
         points.reshape(ngx, CAP, L),
-        used,
+        voxels.reshape(ngx, CAP).T,
+        counts.reshape(1, ngx),
         occupancy.reshape(2),
         weight,
-        w_in,
+        w_in.T,
         cotangent,
+    )
+    steps = 8
+    own = pl.cdiv(ngx, steps)
+    last = ngx // own - 1
+    feat, grad, wgrad = pl.pallas_call(
+        functools.partial(finish, own),
+        grid=(steps,),
+        out_shape=(
+            jax.ShapeDtypeStruct((ngx, CAP, C), BF16),
+            jax.ShapeDtypeStruct((ngx, CAP, L), BF16),
+            jax.ShapeDtypeStruct((27, C, C), F32),
+        ),
+        in_specs=[vmem, vmem, vmem, vmem],
+        out_specs=(
+            pl.BlockSpec((own, CAP, C), lambda i: (jnp.minimum(i, last), 0, 0)),
+            pl.BlockSpec((own, CAP, L), lambda i: (jnp.minimum(i, last), 0, 0)),
+            pl.BlockSpec((4, C, C), lambda i: (jnp.minimum(i, 6), 0, 0)),
+        ),
+    )(
+        *(pltpu.with_memory_space_constraint(x, pltpu.VMEM) for x in (got_y, got_d, summed)),
+        w_in.T,
     )
     return feat[None, None], grad[None, None], wgrad
 

time: 83.4 us -> 69.2 us (0.83)
  local copies, waits for them, and re-layouts: 7.78 us -> 0 us
  Pallas kernels: 73.9 us -> 68.4 us
    unnamed x7 -> x0, local copies, waits for them, and re-layouts: 7.15 us -> none
    pallas_call x1 -> x2, Pallas kernels: 73.9 us -> 68.4 us  [the longest x1 63.7 us: on_device(): pl.pallas_call(functools.partial(kernel, ngx, ngy, pz), out_shape=(pltpu....]
where the time goes in v2:
time: 69.2 us; the launch traced here: 69 us
  Pallas kernels  68.4 us (99%)
    pallas_call x1, Pallas kernels, on_device(): pl.pallas_call(functools.partial(kernel, ngx, ngy, pz), out_shape=(pltpu....  63.7 us
    pallas_call x1, Pallas kernels, on_device(): pl.pallas_call(functools.partial(finish, own), grid=(steps,), out_shape=(...  4.69 us

profile of v2, /device:TPU:1, one launch (start us, length us, event | category | flops | bytes accessed | tf_op | source)
XLA Modules:
  0.0 69.0 jit_solution(1977151665163714720)
XLA Ops:
  0.6 63.7 %shard_map.94 = (bf16[64,24,128]{2,1,0:T(8,128)(2,1)S(1)}, bf16[64,24,128]{2,1,0:T(8,128)(2,1)S(1)}, bf16[32,2,32,128]{3,2,1,0:T(8,128)(2,1)S(1)}) custom-call(bf16[64,32,128]{2,1,0:T(8,128)(2,1)} %bitcast.9, s32[32,64]{1,0:T(8,128)} %bitcast.12, s32[1,64]{1,0:T(1,128)} %bitcast.13, s32[2]{0:T(128)} %bitcast.14, bf16[27,96,96]{2,1,0:T(8,128)(2,1)} %weight.1, ...), custom_call_target="tpu_custom_call" | custom-call | tf_op jit(solution)/shard_map/pallas_call | solution.py:489
  64.3 4.7 %shard_map.95 = (bf16[64,32,96]{2,1,0:T(8,128)(2,1)}, bf16[64,32,128]{2,1,0:T(8,128)(2,1)}, f32[27,96,96]{2,1,0:T(8,128)}) custom-call(bf16[64,24,128]{2,1,0:T(8,128)(2,1)S(1)} %get-tuple-element.9.got_y, bf16[64,24,128]{2,1,0:T(8,128)(2,1)S(1)} %get-tuple-element.10.got_d, bf16[32,2,32,128]{3,2,1,0:T(8,128)(2,1)S(1)} %get-tuple-element.11.summed, ...), custom_call_target="tpu_custom_call" | custom-call | tf_op jit(solution)/shard_map/pallas_call | solution.py:536

commit v3 on v2

--- a/solution.py
+++ b/solution.py
@@ -57,16 +57,24 @@
     ngx,
     ngy,
     pz,
+    pts_in,
+    voxels_in,
+    counts_in,
+    occ,
+    weight_in,
+    w_in_t,
+    cot_in,
+    feat,
+    grad,
+    ag_buf,
     pts,
     voxels_t,
     counts,
-    occ,
     weight,
-    w_in_t,
     cot,
+    in_sem,
     got_y,
     got_d,
-    ag_buf,
     vox,
     rows_p,
     got_p,
@@ -114,6 +122,22 @@
     slot = xy * ngy + gy
     rows = ngx * CAP
 
+    wint[C:L, :] = jnp.zeros((L - C, L), BF16)
+    fetches = [
+        pltpu.make_async_copy(src, dst, in_sem.at[n])
+        for n, (src, dst) in enumerate(
+            (
+                (voxels_in, voxels_t),
+                (counts_in, counts),
+                (cot_in, cot),
+                (w_in_t, wint.at[pl.ds(0, C)]),
+                (pts_in, pts),
+                (weight_in, weight),
+            )
+        )
+    ]
+    for fetch in fetches:
+        fetch.start()
     gpad[...] = jnp.zeros_like(gpad)
     fpad[...] = jnp.zeros_like(fpad)
 
@@ -151,6 +175,8 @@
         def _():
             greet(gx + dx, gy + dy)
 
+    fetches[0].wait()
+    fetches[1].wait()
     used = jnp.where(
         lax.broadcasted_iota(jnp.int32, (CAP, ngx), 0) < counts[...], voxels_t[...], -32
     ).astype(F32)
@@ -159,6 +185,7 @@
         used = jnp.concatenate([used, jnp.zeros((L, L - ngx), F32)], axis=1)
     vox[...] = jnp.transpose(used)[:ngx].astype(jnp.int32).reshape(ngx, 1, L)
 
+    fetches[2].wait()
     o0 = occ[0].astype(F32)
     o1 = occ[1].astype(F32)
 
@@ -168,30 +195,33 @@
         z = lax.broadcasted_iota(jnp.int32, value.shape, 1)
         gpad[x + 1, pl.ds(1, 8), :, pl.ds(0, C)] = (value * jnp.where(z < 8, o0, o1)).astype(BF16)
 
-    wf[...] = jnp.zeros_like(wf)
-    wb[...] = jnp.zeros_like(wb)
-    for tap in range(27):
-        ab, c = tap // 3, tap % 3
-        value = weight[tap]
-        wf[ab * L : ab * L + C, c * L : c * L + C] = value
-        wb[c * L : c * L + C, ab * L : ab * L + C] = value
-    wint[...] = jnp.zeros_like(wint)
-    wint[0:C, :] = w_in_t[...]
-
-    group = min(512, rows)
-    own = group // CAP
-
-    @pl.loop(0, rows // group)
-    def _(i):
-        part = pl.ds(i * own, own)
-        value = dot_nt(pts[part].reshape(group, L), wint[...])
-        rows_p[part] = pack(value, own).astype(BF16)
-
-
     corners = sum(
         (exists(dx, dy).astype(jnp.int32) for dx, dy in directions[4:]), jnp.int32(0)
     )
     pl.semaphore_wait(barrier, (ngx - 1) + pz * (ngy - 1) + corners)
+
+    group = min(512, rows)
+    own = group // CAP
+    groups = ngx // own
+
+    def base_of(i):
+        return lax.rem(gx // own + i, groups) * own
+
+    def exchange_group(src, dst, send, recv, base):
+        @pl.loop(0, own)
+        def _(k):
+            peer = base + lax.rem(gx + k, own)
+
+            @pl.when(peer != gx)
+            def _():
+                pltpu.make_async_remote_copy(
+                    src_ref=src.at[peer],
+                    dst_ref=dst.at[gx],
+                    send_sem=send,
+                    recv_sem=recv,
+                    device_id=(peer, gy),
+                    device_id_type=MESH,
+                ).start()
 
     def exchange(src, dst, send, recv):
         @pl.loop(1, ngx)
@@ -259,9 +289,27 @@
 
     exchange(vox, got_vox, vox_s, vox_r)
     halo_start(gpad, g_s, g_r)
-    exchange(rows_p, got_p, pts_s, pts_r)
+    fetches[3].wait()
+    fetches[4].wait()
+
+    @pl.loop(0, groups)
+    def _(i):
+        base = base_of(i)
+        part = pl.ds(base, own)
+        rows_p[part] = pack(dot_nt(pts[part].reshape(group, L), wint[...]), own).astype(BF16)
+        exchange_group(rows_p, got_p, pts_s, pts_r, base)
+
     got_vox[gx] = vox[gx]
     got_p[gx] = rows_p[gx]
+
+    fetches[5].wait()
+    wf[...] = jnp.zeros_like(wf)
+    wb[...] = jnp.zeros_like(wb)
+    for tap in range(27):
+        ab, c = tap // 3, tap % 3
+        value = weight[tap]
+        wf[ab * L : ab * L + C, c * L : c * L + C] = value
+        wb[c * L : c * L + C, ab * L : ab * L + C] = value
 
     def lift(total, lower, upper):
         count = total.shape[0]
@@ -312,13 +360,14 @@
                 wanted == lane + float(j * L), 1.0, 0.0
             ).astype(BF16)
 
-    def gather(field, out):
-        @pl.loop(0, rows // group)
-        def _(i):
-            got = dot(oht[pl.ds(pl.multiple_of(i * group, group), group), :], field[...])
-            out[pl.ds(i * own, own)] = pack(got, own).astype(BF16)
-
-    gather(field_d, rows_d)
+    def gather(field, out, base):
+        at = pl.ds(pl.multiple_of(base * CAP, group), group)
+        out[pl.ds(base, own)] = pack(dot(oht[at, :], field[...]), own).astype(BF16)
+
+    @pl.loop(0, groups)
+    def _(i):
+        gather(field_d, rows_d, i * own)
+
 
     whole(got_p, ngx - 1, pts_s, pts_r).wait_recv()
 
@@ -399,10 +448,6 @@
         out = lift(z3[:, L : 2 * L], z3[:, :L], z3[:, 2 * L :])
         field_y[pl.ds(pl.multiple_of(i * step * L, step * L), step * L), :] = out.astype(BF16)
 
-    gather(field_y, rows_y)
-    exchange(rows_y, got_y, y_s, y_r)
-    got_y[gx] = rows_y[gx]
-
     whole(rs_buf, plane - 1, rs_s, rs_r).wait_recv()
     total = rs_buf[0].astype(F32)
     for k in range(1, plane):
@@ -421,6 +466,14 @@
             device_id_type=MESH,
         ).start()
 
+    @pl.loop(0, groups)
+    def _(i):
+        base = base_of(i)
+        gather(field_y, rows_y, base)
+        exchange_group(rows_y, got_y, y_s, y_r, base)
+
+    got_y[gx] = rows_y[gx]
+
     whole(z_buf, nz - 1, z_s, z_r).wait_recv()
     total = z_buf[0].astype(F32)
     for k in range(1, nz):
@@ -440,7 +493,21 @@
         ).start()
 
     whole(got_d, ngx - 1, d_s, d_r).wait_recv()
+
+    @pl.loop(0, groups)
+    def _(i):
+        part = pl.ds(i * own, own)
+        value = unpack(got_d[part].astype(F32), own).astype(BF16)
+        grad[part] = dot(value, wint[...]).astype(BF16).reshape(own, CAP, L)
+
     whole(got_y, ngx - 1, y_s, y_r).wait_recv()
+
+    @pl.loop(0, groups)
+    def _(i):
+        part = pl.ds(i * own, own)
+        value = unpack(got_y[part].astype(F32), own).astype(BF16)
+        feat[part] = value[:, :C].reshape(own, CAP, C)
+
     whole(ag_buf, plane - 1, ag_s, ag_r).wait_recv()
 
     whole(vox, ngx - 1, vox_s, vox_r).wait_send()
@@ -454,30 +521,34 @@
     halo_sent(fpad, f_s, f_r)
 
 
-def finish(own, got_y, got_d, summed, w_in_t, feat_out, grad_out, wgrad_out):
-    step = pl.program_id(0)
-    part = pl.ds(jnp.minimum(step, got_y.shape[0] // own - 1) * own, own)
-    feat = unpack(got_y[part].astype(F32), own).astype(BF16)
-    feat_out[...] = feat[:, :C].reshape(own, CAP, C)
-    grad = unpack(got_d[part].astype(F32), own)[:, :C].astype(BF16)
-    grad_out[...] = dot(grad, w_in_t[...]).astype(BF16).reshape(own, CAP, L)
-
+def finish(feat, grad, summed, feat_out, grad_out, wgrad_out, wgrad, sem):
+    copies = [
+        pltpu.make_async_copy(src, dst, sem.at[n])
+        for n, (src, dst) in enumerate(((feat, feat_out), (grad, grad_out)))
+    ]
+    for copy in copies:
+        copy.start()
+    sub = summed.shape[1]
     lane = lax.broadcasted_iota(jnp.int32, (C, L), 1)
-    first = 9 * jnp.minimum(step, 6)
-    sub = summed.shape[1]
-    blocks = [
-        jnp.concatenate(
-            [summed[(first + r) // sub, lax.rem(first + r, sub)] for r in range(3 * j, 3 * j + 3)]
-        ).astype(F32)
-        for j in range(3)
-    ]
-    for j in range(3):
-        wgrad_out[j] = blocks[j][:, :C]
-    last = pltpu.roll(blocks[0], 32, 1)
-    for j in (1, 2):
-        moved = pltpu.roll(blocks[j], 32 + 32 * j, 1)
-        last = jnp.where(lane >= 32 * j, moved, last)
-    wgrad_out[3] = last[:, :C]
+    for g in range(7):
+        blocks = []
+        for j in range(3):
+            first = 9 * g + 3 * j
+            parts = [summed[r // sub, r % sub] for r in range(first, first + 3)]
+            blocks.append(jnp.concatenate(parts).astype(F32))
+            wgrad[4 * g + j] = blocks[j][:, :C]
+        count = 3
+        if g < 6:
+            last = pltpu.roll(blocks[0], 32, 1)
+            for j in (1, 2):
+                last = jnp.where(lane >= 32 * j, pltpu.roll(blocks[j], 32 + 32 * j, 1), last)
+            wgrad[4 * g + 3] = last[:, :C]
+            count = 4
+        part = pl.ds(4 * g, count)
+        copies.append(pltpu.make_async_copy(wgrad.at[part], wgrad_out.at[part], sem.at[2 + g]))
+        copies[-1].start()
+    for copy in copies:
+        copy.wait()
 
 
 def on_device(ngx, ngy, pz, points, counts, voxels, occupancy, weight, w_in, cotangent):
@@ -485,17 +556,26 @@
     nz = ngx // pz
     plane = pz * ngy
     vmem = pl.BlockSpec(memory_space=pltpu.VMEM)
+    place = pl.BlockSpec(memory_space=pl.ANY)
     dma = pltpu.SemaphoreType.DMA
-    got_y, got_d, summed = pl.pallas_call(
+    feat, grad, summed = pl.pallas_call(
         functools.partial(kernel, ngx, ngy, pz),
         out_shape=(
+            pltpu.VMEM((ngx, CAP, C), BF16),
+            pltpu.VMEM((ngx, CAP, L), BF16),
+            pltpu.VMEM((plane, SUB // plane, CAP, L), BF16),
+        ),
+        in_specs=[place, place, place, pl.BlockSpec(memory_space=pltpu.SMEM), place, place, place],
+        out_specs=(vmem, vmem, vmem),
+        scratch_shapes=[
+            pltpu.VMEM((ngx, CAP, L), BF16),
+            pltpu.VMEM((CAP, ngx), jnp.int32),
+            pltpu.VMEM((1, ngx), jnp.int32),
+            pltpu.VMEM((27, C, C), BF16),
+            pltpu.VMEM((8, 8, 16, C), BF16),
+            dma((6,)),
             pltpu.VMEM((ngx, PACK, L), BF16),
             pltpu.VMEM((ngx, PACK, L), BF16),
-            pltpu.VMEM((plane, SUB // plane, CAP, L), BF16),
-        ),
-        in_specs=[vmem, vmem, vmem, pl.BlockSpec(memory_space=pltpu.SMEM), vmem, vmem, vmem],
-        out_specs=(vmem, vmem, vmem),
-        scratch_shapes=[
             pltpu.VMEM((ngx, 1, L), jnp.int32),
             pltpu.VMEM((ngx, PACK, L), BF16),
             pltpu.VMEM((ngx, PACK, L), BF16),
@@ -530,27 +610,18 @@
         w_in.T,
         cotangent,
     )
-    steps = 8
-    own = pl.cdiv(ngx, steps)
-    last = ngx // own - 1
+    return_shape = (
+        jax.ShapeDtypeStruct((ngx, CAP, C), BF16),
+        jax.ShapeDtypeStruct((ngx, CAP, L), BF16),
+        jax.ShapeDtypeStruct((27, C, C), F32),
+    )
     feat, grad, wgrad = pl.pallas_call(
-        functools.partial(finish, own),
-        grid=(steps,),
-        out_shape=(
-            jax.ShapeDtypeStruct((ngx, CAP, C), BF16),
-            jax.ShapeDtypeStruct((ngx, CAP, L), BF16),
-            jax.ShapeDtypeStruct((27, C, C), F32),
-        ),
-        in_specs=[vmem, vmem, vmem, vmem],
-        out_specs=(
-            pl.BlockSpec((own, CAP, C), lambda i: (jnp.minimum(i, last), 0, 0)),
-            pl.BlockSpec((own, CAP, L), lambda i: (jnp.minimum(i, last), 0, 0)),
-            pl.BlockSpec((4, C, C), lambda i: (jnp.minimum(i, 6), 0, 0)),
-        ),
-    )(
-        *(pltpu.with_memory_space_constraint(x, pltpu.VMEM) for x in (got_y, got_d, summed)),
-        w_in.T,
-    )
+        finish,
+        out_shape=return_shape,
+        in_specs=[vmem, vmem, vmem],
+        out_specs=(place, place, place),
+        scratch_shapes=[pltpu.VMEM((27, C, C), F32), dma((9,))],
+    )(*(pltpu.with_memory_space_constraint(x, pltpu.VMEM) for x in (feat, grad, summed)))
     return feat[None, None], grad[None, None], wgrad
 
 

time: 69.2 us -> 63.2 us (0.913)
  Pallas kernels: 68.4 us -> 62.5 us
    pallas_call x1, Pallas kernels: 4.69 us -> 1.47 us  [on_device(): pl.pallas_call(finish, out_shape=return_shape, in_specs=[vmem, vmem, vmem...]
    pallas_call x1, Pallas kernels: 63.7 us -> 61 us  [on_device(): pl.pallas_call(functools.partial(kernel, ngx, ngy, pz), out_shape=(pltpu....]
where the time goes in v3:
time: 63.2 us; the launch traced here: 63.1 us
  Pallas kernels  62.5 us (99%)
  between operations  0.64 us (1%)
    pallas_call x1, Pallas kernels, on_device(): pl.pallas_call(functools.partial(kernel, ngx, ngy, pz), out_shape=(pltpu....  61 us
    pallas_call x1, Pallas kernels, on_device(): pl.pallas_call(finish, out_shape=return_shape, in_specs=[vmem, vmem, vmem...  1.47 us

profile of v3, /device:TPU:1, one launch (start us, length us, event | category | flops | bytes accessed | tf_op | source)
XLA Modules:
  0.0 63.1 jit_solution(13568166733881263679)
XLA Ops:
  0.6 61.0 %shard_map.94 = (bf16[64,32,96]{2,1,0:T(8,128)(2,1)S(1)}, bf16[64,32,128]{2,1,0:T(8,128)(2,1)S(1)}, bf16[32,2,32,128]{3,2,1,0:T(8,128)(2,1)S(1)}) custom-call(bf16[64,32,128]{2,1,0:T(8,128)(2,1)} %bitcast.9, s32[32,64]{1,0:T(8,128)} %bitcast.11, s32[1,64]{1,0:T(1,128)} %bitcast.12, s32[2]{0:T(128)} %bitcast.13, bf16[27,96,96]{2,1,0:T(8,128)(2,1)} %weight_in.1, ...), custom_call_target="tpu_custom_call" | custom-call | tf_op jit(solution)/shard_map/pallas_call | solution.py:561
  61.7 1.5 %shard_map.95 = (bf16[64,32,96]{2,1,0:T(8,128)(2,1)}, bf16[64,32,128]{2,1,0:T(8,128)(2,1)}, f32[27,96,96]{2,1,0:T(8,128)}) custom-call(bf16[64,32,96]{2,1,0:T(8,128)(2,1)S(1)} %get-tuple-element.9.feat, bf16[64,32,128]{2,1,0:T(8,128)(2,1)S(1)} %get-tuple-element.10.grad, bf16[32,2,32,128]{3,2,1,0:T(8,128)(2,1)S(1)} %get-tuple-element.11.summed), custom_call_target="tpu_custom_call" | custom-call | tf_op jit(solution)/shard_map/pallas_call | solution.py:618

commit v4 on v3

--- a/solution.py
+++ b/solution.py
@@ -92,6 +92,8 @@
     field_y,
     wg,
     pk,
+    pair_buf,
+    rs_src,
     rs_buf,
     z_buf,
     vox_s,
@@ -112,14 +114,21 @@
     g_r,
     f_s,
     f_r,
+    pair_s,
+    pair_r,
+    swap_s,
+    swap_r,
 ):
     gx = lax.axis_index("gx")
     gy = lax.axis_index("gy")
     nz = ngx // pz
-    plane = pz * ngy
+    half = SUB // 2
+    lanes = ngy // 2
+    plane = pz * lanes
     zi = gx // pz
     xy = lax.rem(gx, pz)
-    slot = xy * ngy + gy
+    core = lax.rem(gy, 2)
+    slot = xy * lanes + gy // 2
     rows = ngx * CAP
 
     wint[C:L, :] = jnp.zeros((L - C, L), BF16)
@@ -297,8 +306,8 @@
         base = base_of(i)
         part = pl.ds(base, own)
         rows_p[part] = pack(dot_nt(pts[part].reshape(group, L), wint[...]), own).astype(BF16)
-        exchange_group(rows_p, got_p, pts_s, pts_r, base)
-
+
+    exchange(rows_p, got_p, pts_s, pts_r)
     got_vox[gx] = vox[gx]
     got_p[gx] = rows_p[gx]
 
@@ -417,21 +426,38 @@
             pk[9 * g + 3 * j : 9 * g + 3 * j + 3] = block.astype(BF16).reshape(3, CAP, L)
     pk[63] = jnp.zeros((CAP, L), BF16)
 
-    sub = SUB // plane
+    sub = half // plane
+    sibling = (gx, gy + 1 - 2 * core)
+
+    def plane_peer(peer):
+        return (zi * pz + peer // lanes, lax.rem(peer, lanes) * 2 + core)
+
+    pair = pltpu.make_async_remote_copy(
+        src_ref=pk.at[pl.ds((1 - core) * half, half)],
+        dst_ref=pair_buf,
+        send_sem=pair_s,
+        recv_sem=pair_r,
+        device_id=sibling,
+        device_id_type=MESH,
+    )
+    pair.start()
+    pair.wait_recv()
+    both = pk[pl.ds(core * half, half)].astype(F32) + pair_buf[...].astype(F32)
+    rs_src[...] = both.astype(BF16)
 
     @pl.loop(1, plane)
     def _(k):
         peer = lax.rem(slot + k, plane)
         pltpu.make_async_remote_copy(
-            src_ref=pk.at[pl.ds(peer * sub, sub)],
+            src_ref=rs_src.at[pl.ds(peer * sub, sub)],
             dst_ref=rs_buf.at[slot],
             send_sem=rs_s,
             recv_sem=rs_r,
-            device_id=(zi * pz + peer // ngy, lax.rem(peer, ngy)),
+            device_id=plane_peer(peer),
             device_id_type=MESH,
         ).start()
 
-    rs_buf[slot] = pk[pl.ds(slot * sub, sub)]
+    rs_buf[slot] = rs_src[pl.ds(slot * sub, sub)]
     exchange(rows_d, got_d, d_s, d_r)
     got_d[gx] = rows_d[gx]
 
@@ -470,25 +496,26 @@
     def _(i):
         base = base_of(i)
         gather(field_y, rows_y, base)
-        exchange_group(rows_y, got_y, y_s, y_r, base)
-
+
+    exchange(rows_y, got_y, y_s, y_r)
     got_y[gx] = rows_y[gx]
 
     whole(z_buf, nz - 1, z_s, z_r).wait_recv()
     total = z_buf[0].astype(F32)
     for k in range(1, nz):
         total = total + z_buf[k].astype(F32)
-    ag_buf[slot] = total.astype(BF16)
+    mine = ag_buf.at[core]
+    mine[slot] = total.astype(BF16)
 
     @pl.loop(1, plane)
     def _(k):
         peer = lax.rem(slot + k, plane)
         pltpu.make_async_remote_copy(
-            src_ref=ag_buf.at[slot],
-            dst_ref=ag_buf.at[slot],
+            src_ref=mine.at[slot],
+            dst_ref=mine.at[slot],
             send_sem=ag_s,
             recv_sem=ag_r,
-            device_id=(zi * pz + peer // ngy, lax.rem(peer, ngy)),
+            device_id=plane_peer(peer),
             device_id_type=MESH,
         ).start()
 
@@ -508,7 +535,17 @@
         value = unpack(got_y[part].astype(F32), own).astype(BF16)
         feat[part] = value[:, :C].reshape(own, CAP, C)
 
-    whole(ag_buf, plane - 1, ag_s, ag_r).wait_recv()
+    whole(mine, plane - 1, ag_s, ag_r).wait_recv()
+    swap = pltpu.make_async_remote_copy(
+        src_ref=mine,
+        dst_ref=mine,
+        send_sem=swap_s,
+        recv_sem=swap_r,
+        device_id=sibling,
+        device_id_type=MESH,
+    )
+    swap.start()
+    swap.wait_recv()
 
     whole(vox, ngx - 1, vox_s, vox_r).wait_send()
     whole(rows_p, ngx - 1, pts_s, pts_r).wait_send()
@@ -516,7 +553,9 @@
     whole(rows_y, ngx - 1, y_s, y_r).wait_send()
     whole(rs_buf, plane - 1, rs_s, rs_r).wait_send()
     whole(z_buf, nz - 1, z_s, z_r).wait_send()
-    whole(ag_buf, plane - 1, ag_s, ag_r).wait_send()
+    whole(mine, plane - 1, ag_s, ag_r).wait_send()
+    pair.wait_send()
+    swap.wait_send()
     halo_sent(gpad, g_s, g_r)
     halo_sent(fpad, f_s, f_r)
 
@@ -528,13 +567,16 @@
     ]
     for copy in copies:
         copy.start()
-    sub = summed.shape[1]
+    plane, sub = summed.shape[1:3]
+    half = plane * sub
     lane = lax.broadcasted_iota(jnp.int32, (C, L), 1)
     for g in range(7):
         blocks = []
         for j in range(3):
             first = 9 * g + 3 * j
-            parts = [summed[r // sub, r % sub] for r in range(first, first + 3)]
+            parts = [
+                summed[r // half, r % half // sub, r % sub] for r in range(first, first + 3)
+            ]
             blocks.append(jnp.concatenate(parts).astype(F32))
             wgrad[4 * g + j] = blocks[j][:, :C]
         count = 3
@@ -554,7 +596,8 @@
 def on_device(ngx, ngy, pz, points, counts, voxels, occupancy, weight, w_in, cotangent):
     rows = ngx * CAP
     nz = ngx // pz
-    plane = pz * ngy
+    plane = pz * (ngy // 2)
+    half = SUB // 2
     vmem = pl.BlockSpec(memory_space=pltpu.VMEM)
     place = pl.BlockSpec(memory_space=pl.ANY)
     dma = pltpu.SemaphoreType.DMA
@@ -563,7 +606,7 @@
         out_shape=(
             pltpu.VMEM((ngx, CAP, C), BF16),
             pltpu.VMEM((ngx, CAP, L), BF16),
-            pltpu.VMEM((plane, SUB // plane, CAP, L), BF16),
+            pltpu.VMEM((2, plane, half // plane, CAP, L), BF16),
         ),
         in_specs=[place, place, place, pl.BlockSpec(memory_space=pltpu.SMEM), place, place, place],
         out_specs=(vmem, vmem, vmem),
@@ -593,11 +636,14 @@
             pltpu.VMEM((NV, L), BF16),
             pltpu.VMEM((3 * C, 9 * L), F32),
             pltpu.VMEM((SUB, CAP, L), BF16),
-            pltpu.VMEM((plane, SUB // plane, CAP, L), BF16),
-            pltpu.VMEM((nz, SUB // plane, CAP, L), BF16),
+            pltpu.VMEM((half, CAP, L), BF16),
+            pltpu.VMEM((half, CAP, L), BF16),
+            pltpu.VMEM((plane, half // plane, CAP, L), BF16),
+            pltpu.VMEM((nz, half // plane, CAP, L), BF16),
         ]
         + [dma] * 14
-        + [dma((8,))] * 4,
+        + [dma((8,))] * 4
+        + [dma] * 4,
         compiler_params=pltpu.CompilerParams(
             collective_id=0, has_side_effects=True, vmem_limit_bytes=56 * 1024 * 1024
         ),

time: 63.2 us -> 61 us (0.965)
  Pallas kernels: 62.5 us -> 60.2 us
    pallas_call x1, Pallas kernels: 61 us -> 58.8 us  [on_device(): pl.pallas_call(functools.partial(kernel, ngx, ngy, pz), out_shape=(pltpu....]
where the time goes in v4:
time: 61 us; the launch traced here: 60.9 us
  Pallas kernels  60.2 us (99%)
  between operations  0.64 us (1%)
    pallas_call x1, Pallas kernels, on_device(): pl.pallas_call(functools.partial(kernel, ngx, ngy, pz), out_shape=(pltpu....  58.8 us
    pallas_call x1, Pallas kernels, on_device(): pl.pallas_call(finish, out_shape=return_shape, in_specs=[vmem, vmem, vmem...  1.47 us

profile of v4, /device:TPU:1, one launch (start us, length us, event | category | flops | bytes accessed | tf_op | source)
XLA Modules:
  0.0 60.9 jit_solution(13711151126784339323)
XLA Ops:
  0.6 58.8 %shard_map.94 = (bf16[64,32,96]{2,1,0:T(8,128)(2,1)S(1)}, bf16[64,32,128]{2,1,0:T(8,128)(2,1)S(1)}, bf16[2,16,2,32,128]{4,3,2,1,0:T(8,128)(2,1)S(1)}) custom-call(bf16[64,32,128]{2,1,0:T(8,128)(2,1)} %bitcast.9, s32[32,64]{1,0:T(8,128)} %bitcast.11, s32[1,64]{1,0:T(1,128)} %bitcast.12, s32[2]{0:T(128)} %bitcast.13, bf16[27,96,96]{2,1,0:T(8,128)(2,1)} %weight_in.1, ...), custom_call_target="tpu_custom_call" | custom-call | tf_op jit(solution)/shard_map/pallas_call | solution.py:604
  59.4 1.5 %shard_map.95 = (bf16[64,32,96]{2,1,0:T(8,128)(2,1)}, bf16[64,32,128]{2,1,0:T(8,128)(2,1)}, f32[27,96,96]{2,1,0:T(8,128)}) custom-call(bf16[64,32,96]{2,1,0:T(8,128)(2,1)S(1)} %get-tuple-element.9.feat, bf16[64,32,128]{2,1,0:T(8,128)(2,1)S(1)} %get-tuple-element.10.grad, bf16[2,16,2,32,128]{4,3,2,1,0:T(8,128)(2,1)S(1)} %get-tuple-element.11.summed), custom_call_target="tpu_custom_call" | custom-call | tf_op jit(solution)/shard_map/pallas_call | solution.py:664

commit v5 on v4

--- a/solution.py
+++ b/solution.py
@@ -78,7 +78,7 @@
     vox,
     rows_p,
     got_p,
-    proj,
+    acc,
     got_vox,
     rows_d,
     rows_y,
@@ -204,33 +204,22 @@
         z = lax.broadcasted_iota(jnp.int32, value.shape, 1)
         gpad[x + 1, pl.ds(1, 8), :, pl.ds(0, C)] = (value * jnp.where(z < 8, o0, o1)).astype(BF16)
 
-    corners = sum(
-        (exists(dx, dy).astype(jnp.int32) for dx, dy in directions[4:]), jnp.int32(0)
-    )
-    pl.semaphore_wait(barrier, (ngx - 1) + pz * (ngy - 1) + corners)
-
     group = min(512, rows)
     own = group // CAP
     groups = ngx // own
 
-    def base_of(i):
-        return lax.rem(gx // own + i, groups) * own
-
-    def exchange_group(src, dst, send, recv, base):
-        @pl.loop(0, own)
-        def _(k):
-            peer = base + lax.rem(gx + k, own)
-
-            @pl.when(peer != gx)
-            def _():
-                pltpu.make_async_remote_copy(
-                    src_ref=src.at[peer],
-                    dst_ref=dst.at[gx],
-                    send_sem=send,
-                    recv_sem=recv,
-                    device_id=(peer, gy),
-                    device_id_type=MESH,
-                ).start()
+    fetches[3].wait()
+    fetches[4].wait()
+
+    @pl.loop(0, groups)
+    def _(i):
+        part = pl.ds(i * own, own)
+        rows_p[part] = pack(dot_nt(pts[part].reshape(group, L), wint[...]), own).astype(BF16)
+
+    corners = sum(
+        (exists(dx, dy).astype(jnp.int32) for dx, dy in directions[4:]), jnp.int32(0)
+    )
+    pl.semaphore_wait(barrier, (ngx - 1) + pz * (ngy - 1) + corners)
 
     def exchange(src, dst, send, recv):
         @pl.loop(1, ngx)
@@ -298,16 +287,7 @@
 
     exchange(vox, got_vox, vox_s, vox_r)
     halo_start(gpad, g_s, g_r)
-    fetches[3].wait()
-    fetches[4].wait()
-
-    @pl.loop(0, groups)
-    def _(i):
-        base = base_of(i)
-        part = pl.ds(base, own)
-        rows_p[part] = pack(dot_nt(pts[part].reshape(group, L), wint[...]), own).astype(BF16)
-
-    exchange(rows_p, got_p, pts_s, pts_r)
+    exchange(rows_p, got_p, pts_s, pts_r.at[gx // own])
     got_vox[gx] = vox[gx]
     got_p[gx] = rows_p[gx]
 
@@ -378,20 +358,23 @@
         gather(field_d, rows_d, i * own)
 
 
-    whole(got_p, ngx - 1, pts_s, pts_r).wait_recv()
-
-    @pl.loop(0, rows // group)
-    def _(i):
-        value = unpack(got_p[pl.ds(i * own, own)].astype(F32), own)
-        proj[pl.ds(pl.multiple_of(i * group, group), group), :] = value.astype(BF16)
-
     eye = jnp.where(
         lax.broadcasted_iota(jnp.int32, (L, L), 0) == lax.broadcasted_iota(jnp.int32, (L, L), 1),
         1.0,
         0.0,
     ).astype(BF16)
-    proj_t = dot_nt(eye, proj[...]).astype(BF16)
-    sum_t = dot(proj_t, oht[...])
+
+    for i in range(1, groups + 1):
+        source = lax.rem(gx // own + groups - i, groups)
+        expected = own if i < groups else own - 1
+        whole(got_p, expected, pts_s, pts_r.at[source]).wait_recv()
+        part = pl.ds(source * own, own)
+        at = pl.ds(pl.multiple_of(source * group, group), group)
+        value = unpack(got_p[part].astype(F32), own).astype(BF16)
+        added = dot(dot_nt(eye, value).astype(BF16), oht[at, :])
+        acc[...] = added if i == 1 else acc[...] + added
+
+    sum_t = acc[...]
     z_lane = lax.broadcasted_iota(jnp.int32, sum_t.shape, 1) % 16
     sum_t = (sum_t * jnp.where(z_lane < 8, o0, o1)).astype(BF16).astype(F32)
     f0 = jnp.transpose(sum_t).astype(BF16).reshape(8, 8, 16, L)
@@ -494,8 +477,7 @@
 
     @pl.loop(0, groups)
     def _(i):
-        base = base_of(i)
-        gather(field_y, rows_y, base)
+        gather(field_y, rows_y, i * own)
 
     exchange(rows_y, got_y, y_s, y_r)
     got_y[gx] = rows_y[gx]
@@ -548,7 +530,7 @@
     swap.wait_recv()
 
     whole(vox, ngx - 1, vox_s, vox_r).wait_send()
-    whole(rows_p, ngx - 1, pts_s, pts_r).wait_send()
+    whole(rows_p, ngx - 1, pts_s, pts_r.at[0]).wait_send()
     whole(rows_d, ngx - 1, d_s, d_r).wait_send()
     whole(rows_y, ngx - 1, y_s, y_r).wait_send()
     whole(rs_buf, plane - 1, rs_s, rs_r).wait_send()
@@ -622,7 +604,7 @@
             pltpu.VMEM((ngx, 1, L), jnp.int32),
             pltpu.VMEM((ngx, PACK, L), BF16),
             pltpu.VMEM((ngx, PACK, L), BF16),
-            pltpu.VMEM((rows, L), BF16),
+            pltpu.VMEM((L, NV), F32),
             pltpu.VMEM((ngx, 1, L), jnp.int32),
             pltpu.VMEM((ngx, PACK, L), BF16),
             pltpu.VMEM((ngx, PACK, L), BF16),
@@ -641,7 +623,9 @@
             pltpu.VMEM((plane, half // plane, CAP, L), BF16),
             pltpu.VMEM((nz, half // plane, CAP, L), BF16),
         ]
-        + [dma] * 14
+        + [dma] * 3
+        + [dma((pl.cdiv(ngx, 16),))]
+        + [dma] * 10
         + [dma((8,))] * 4
         + [dma] * 4,
         compiler_params=pltpu.CompilerParams(

time: 61 us -> 63.5 us (1.041)
  Pallas kernels: 60.2 us -> 62.8 us
    pallas_call x1, Pallas kernels: 58.8 us -> 61.3 us  [on_device(): pl.pallas_call(functools.partial(kernel, ngx, ngy, pz), out_shape=(pltpu....]
where the time goes in v5:
time: 63.5 us; the launch traced here: 63.4 us
  Pallas kernels  62.8 us (99%)
  between operations  0.64 us (1%)
    pallas_call x1, Pallas kernels, on_device(): pl.pallas_call(functools.partial(kernel, ngx, ngy, pz), out_shape=(pltpu....  61.3 us
    pallas_call x1, Pallas kernels, on_device(): pl.pallas_call(finish, out_shape=return_shape, in_specs=[vmem, vmem, vmem...  1.47 us

profile of v5, /device:TPU:1, one launch (start us, length us, event | category | flops | bytes accessed | tf_op | source)
XLA Modules:
  0.0 63.4 jit_solution(9825971819434781618)
XLA Ops:
  0.6 61.3 %shard_map.94 = (bf16[64,32,96]{2,1,0:T(8,128)(2,1)S(1)}, bf16[64,32,128]{2,1,0:T(8,128)(2,1)S(1)}, bf16[2,16,2,32,128]{4,3,2,1,0:T(8,128)(2,1)S(1)}) custom-call(bf16[64,32,128]{2,1,0:T(8,128)(2,1)} %bitcast.9, s32[32,64]{1,0:T(8,128)} %bitcast.11, s32[1,64]{1,0:T(1,128)} %bitcast.12, s32[2]{0:T(128)} %bitcast.13, bf16[27,96,96]{2,1,0:T(8,128)(2,1)} %weight_in.1, ...), custom_call_target="tpu_custom_call" | custom-call | tf_op jit(solution)/shard_map/pallas_call | solution.py:586
  62.0 1.5 %shard_map.95 = (bf16[64,32,96]{2,1,0:T(8,128)(2,1)}, bf16[64,32,128]{2,1,0:T(8,128)(2,1)}, f32[27,96,96]{2,1,0:T(8,128)}) custom-call(bf16[64,32,96]{2,1,0:T(8,128)(2,1)S(1)} %get-tuple-element.9.feat, bf16[64,32,128]{2,1,0:T(8,128)(2,1)S(1)} %get-tuple-element.10.grad, bf16[2,16,2,32,128]{4,3,2,1,0:T(8,128)(2,1)S(1)} %get-tuple-element.11.summed), custom_call_target="tpu_custom_call" | custom-call | tf_op jit(solution)/shard_map/pallas_call | solution.py:648

commit v6 on v4

--- a/solution.py
+++ b/solution.py
@@ -78,7 +78,7 @@
     vox,
     rows_p,
     got_p,
-    proj,
+    acc,
     got_vox,
     rows_d,
     rows_y,
@@ -307,7 +307,7 @@
         part = pl.ds(base, own)
         rows_p[part] = pack(dot_nt(pts[part].reshape(group, L), wint[...]), own).astype(BF16)
 
-    exchange(rows_p, got_p, pts_s, pts_r)
+    exchange(rows_p, got_p, pts_s, pts_r.at[gx // own])
     got_vox[gx] = vox[gx]
     got_p[gx] = rows_p[gx]
 
@@ -344,10 +344,10 @@
         field_d[pl.ds(pl.multiple_of(i * step * L, step * L), step * L), :] = out.astype(BF16)
 
     whole(got_vox, ngx - 1, vox_s, vox_r).wait_recv()
-    chunk = min(256, rows)
+    chunk = min(512, rows)
     ids = got_vox[...].reshape(ngx, L)
-    high = (ids >> 5).astype(F32).astype(BF16)
-    low = (ids & 31).astype(F32).astype(BF16)
+    low = pltpu.roll((ids & 31).astype(F32), CAP, 1)
+    digits = ((ids >> 5).astype(F32) + low).astype(BF16)
     ones = jnp.ones((L, L), BF16)
 
     @pl.loop(0, rows // chunk)
@@ -356,13 +356,13 @@
         pick = jnp.where(
             owner == lax.broadcasted_iota(jnp.int32, (chunk, ngx), 1), 1.0, 0.0
         ).astype(BF16)
-        here = (
-            lax.broadcasted_iota(jnp.int32, (chunk, L), 0) % CAP
-            == lax.broadcasted_iota(jnp.int32, (chunk, L), 1)
+        place = lax.broadcasted_iota(jnp.int32, (chunk, L), 0) % CAP
+        column = lax.broadcasted_iota(jnp.int32, (chunk, L), 1)
+        both = dot(pick, digits)
+        both = jnp.where(
+            column == place, both * 32.0, jnp.where(column == place + CAP, both, 0.0)
         )
-        hi = jnp.where(here, dot(pick, high) * 32.0, 0.0).astype(BF16)
-        lo = jnp.where(here, dot(pick, low), 0.0).astype(BF16)
-        wanted = dot(hi, ones) + dot(lo, ones)
+        wanted = dot(both.astype(BF16), ones)
         lane = lax.broadcasted_iota(jnp.int32, (chunk, L), 1).astype(F32)
         for j in range(NV // L):
             oht[pl.ds(pl.multiple_of(i * chunk, chunk), chunk), j * L : (j + 1) * L] = jnp.where(
@@ -378,20 +378,23 @@
         gather(field_d, rows_d, i * own)
 
 
-    whole(got_p, ngx - 1, pts_s, pts_r).wait_recv()
-
-    @pl.loop(0, rows // group)
-    def _(i):
-        value = unpack(got_p[pl.ds(i * own, own)].astype(F32), own)
-        proj[pl.ds(pl.multiple_of(i * group, group), group), :] = value.astype(BF16)
-
     eye = jnp.where(
         lax.broadcasted_iota(jnp.int32, (L, L), 0) == lax.broadcasted_iota(jnp.int32, (L, L), 1),
         1.0,
         0.0,
     ).astype(BF16)
-    proj_t = dot_nt(eye, proj[...]).astype(BF16)
-    sum_t = dot(proj_t, oht[...])
+
+    for i in range(1, groups + 1):
+        source = lax.rem(gx // own + groups - i, groups)
+        expected = own if i < groups else own - 1
+        whole(got_p, expected, pts_s, pts_r.at[source]).wait_recv()
+        part = pl.ds(source * own, own)
+        at = pl.ds(pl.multiple_of(source * group, group), group)
+        value = unpack(got_p[part].astype(F32), own).astype(BF16)
+        added = dot(dot_nt(eye, value).astype(BF16), oht[at, :])
+        acc[...] = added if i == 1 else acc[...] + added
+
+    sum_t = acc[...]
     z_lane = lax.broadcasted_iota(jnp.int32, sum_t.shape, 1) % 16
     sum_t = (sum_t * jnp.where(z_lane < 8, o0, o1)).astype(BF16).astype(F32)
     f0 = jnp.transpose(sum_t).astype(BF16).reshape(8, 8, 16, L)
@@ -548,7 +551,7 @@
     swap.wait_recv()
 
     whole(vox, ngx - 1, vox_s, vox_r).wait_send()
-    whole(rows_p, ngx - 1, pts_s, pts_r).wait_send()
+    whole(rows_p, ngx - 1, pts_s, pts_r.at[0]).wait_send()
     whole(rows_d, ngx - 1, d_s, d_r).wait_send()
     whole(rows_y, ngx - 1, y_s, y_r).wait_send()
     whole(rs_buf, plane - 1, rs_s, rs_r).wait_send()
@@ -622,7 +625,7 @@
             pltpu.VMEM((ngx, 1, L), jnp.int32),
             pltpu.VMEM((ngx, PACK, L), BF16),
             pltpu.VMEM((ngx, PACK, L), BF16),
-            pltpu.VMEM((rows, L), BF16),
+            pltpu.VMEM((L, NV), F32),
             pltpu.VMEM((ngx, 1, L), jnp.int32),
             pltpu.VMEM((ngx, PACK, L), BF16),
             pltpu.VMEM((ngx, PACK, L), BF16),
@@ -641,7 +644,9 @@
             pltpu.VMEM((plane, half // plane, CAP, L), BF16),
             pltpu.VMEM((nz, half // plane, CAP, L), BF16),
         ]
-        + [dma] * 14
+        + [dma] * 3
+        + [dma((pl.cdiv(ngx, 16),))]
+        + [dma] * 10
         + [dma((8,))] * 4
         + [dma] * 4,
         compiler_params=pltpu.CompilerParams(

time: 61 us -> 61 us (level)
  no operation moved by 1% of the time
where the time goes in v6:
time: 61 us; the launch traced here: 60.7 us
  Pallas kernels  60.1 us (99%)
  between operations  0.64 us (1%)
    pallas_call x1, Pallas kernels, on_device(): pl.pallas_call(functools.partial(kernel, ngx, ngy, pz), out_shape=(pltpu....  58.6 us
    pallas_call x1, Pallas kernels, on_device(): pl.pallas_call(finish, out_shape=return_shape, in_specs=[vmem, vmem, vmem...  1.47 us

profile of v6, /device:TPU:1, one launch (start us, length us, event | category | flops | bytes accessed | tf_op | source)
XLA Modules:
  0.0 60.7 jit_solution(590202957977150048)
XLA Ops:
  0.6 58.6 %shard_map.94 = (bf16[64,32,96]{2,1,0:T(8,128)(2,1)S(1)}, bf16[64,32,128]{2,1,0:T(8,128)(2,1)S(1)}, bf16[2,16,2,32,128]{4,3,2,1,0:T(8,128)(2,1)S(1)}) custom-call(bf16[64,32,128]{2,1,0:T(8,128)(2,1)} %bitcast.9, s32[32,64]{1,0:T(8,128)} %bitcast.11, s32[1,64]{1,0:T(1,128)} %bitcast.12, s32[2]{0:T(128)} %bitcast.13, bf16[27,96,96]{2,1,0:T(8,128)(2,1)} %weight_in.1, ...), custom_call_target="tpu_custom_call" | custom-call | tf_op jit(solution)/shard_map/pallas_call | solution.py:607
  59.2 1.5 %shard_map.95 = (bf16[64,32,96]{2,1,0:T(8,128)(2,1)}, bf16[64,32,128]{2,1,0:T(8,128)(2,1)}, f32[27,96,96]{2,1,0:T(8,128)}) custom-call(bf16[64,32,96]{2,1,0:T(8,128)(2,1)S(1)} %get-tuple-element.9.feat, bf16[64,32,128]{2,1,0:T(8,128)(2,1)S(1)} %get-tuple-element.10.grad, bf16[2,16,2,32,128]{4,3,2,1,0:T(8,128)(2,1)S(1)} %get-tuple-element.11.summed), custom_call_target="tpu_custom_call" | custom-call | tf_op jit(solution)/shard_map/pallas_call | solution.py:669
